TPU v7x, 32 devices: a whole 2x2x4 slice. The times are simulated.
32 devices in a mesh: ex: 2 (over x), ey: 2 (over y), lin: 8 (over z, core).
Axes of the slice: x: 2, y: 2, z: 4, core: 2. Of those that a mesh axis runs over, the one named last changes fastest.
Arguments:
- load: float32 [5, 5, 5, 4, 16, 256], P(None, None, None, None, ('ey', 'lin'), 'ex'), may hold values from -6 to 6
- kappa: float32 [4, 16, 256], P(None, ('ey', 'lin'), 'ex'), may hold values from 0.3 to 3
- wet: int32 [4, 16, 256], P(None, ('ey', 'lin'), 'ex'), may hold values 0 or 1
Outputs:
- solution: float32 [5, 5, 5, 4, 16, 256], P(None, None, None, None, ('ey', 'lin'), 'ex')
- residual: float32 [5, 5, 5, 4, 16, 256], P(None, None, None, None, ('ey', 'lin'), 'ex')
All inputs are finite; a program needn't handle non-finite values. No bound on the sum of `wet` on one device may be relied on, other than what follows from the above.
Results may differ from a plain program's by a relative error of at most 0.00016.
Values sent between devices are 32-bit elements; how exact they have to be, the bound alone decides.
A program may use at most 64 MiB of HBM per device.

v0:
```python
import functools
import math

import jax
import jax.numpy as jnp
import numpy as np
from jax import lax
from jax.experimental import pallas as pl
from jax.experimental.pallas import tpu as pltpu
from jax.sharding import PartitionSpec as P

N = 5
CYCLES = 2
NPRE = 2
NPOST = 2
NC = 4
FINE_RELAX = 0.25
COARSE_RELAX = 0.4
REACH = NC + 1
STEPS = CYCLES * (NPRE + NPOST) + 1
HALO = 32
MESH = pl.DeviceIdType.MESH
F32 = jnp.float32


def node_tables():
    points = np.array([-1.0, -math.sqrt(3.0 / 7.0), 0.0, math.sqrt(3.0 / 7.0), 1.0])
    weights = np.array([0.1, 49.0 / 90.0, 32.0 / 45.0, 49.0 / 90.0, 0.1])
    eye_table = np.eye(points.shape[0])
    spread = points[:, None] - points[None, :] + eye_table
    factors = np.prod(spread, axis=1)
    deriv = factors[:, None] / (factors[None, :] * spread)
    deriv = np.where(eye_table > 0, (np.sum(1.0 / spread, axis=1) - 1.0)[:, None], deriv)
    stiff = deriv.T @ (weights[:, None] * deriv)
    mass = eye_table * weights[:, None]
    interp = np.stack([(1.0 - points) / 2.0, (1.0 + points) / 2.0], axis=1)
    return stiff, weights, interp, interp.T @ stiff @ interp, interp.T @ mass @ interp


STIFF, WEIGHTS, INTERP, COARSE_STIFF, COARSE_MASS = node_tables()
D = STIFF / WEIGHTS[:, None]
W3 = WEIGHTS[:, None, None] * WEIGHTS[None, :, None] * WEIGHTS[None, None, :]
DD = np.diag(D)
K3 = W3 * (DD[:, None, None] + DD[None, :, None] + DD[None, None, :])


def node(a, b, c):
    return (a * N + b) * N + c


def line_parts(v):
    twice = v[2] + v[2]
    return (v[0] + v[4]) - twice, (v[1] + v[3]) - twice, v[0] - v[4], v[1] - v[3]


def row_even(i, parts):
    return float((D[i, 0] + D[i, 4]) / 2) * parts[0] + float((D[i, 1] + D[i, 3]) / 2) * parts[1]


def row_odd(i, parts):
    return float((D[i, 0] - D[i, 4]) / 2) * parts[2] + float((D[i, 1] - D[i, 3]) / 2) * parts[3]


def line_apply(v):
    parts = line_parts(v)
    e0, e1, e2 = (row_even(i, parts) for i in range(3))
    o0, o1 = (row_odd(i, parts) for i in range(2))
    return [e0 + o0, e1 + o1, e2, e1 - o1, e0 - o0]


def scaled(factor, value):
    factor = float(factor)
    if factor == 1.0:
        return value
    return factor * value


def mix(pairs):
    total = None
    for factor, value in pairs:
        if abs(float(factor)) < 1e-14:
            continue
        term = scaled(factor, value)
        total = term if total is None else total + term
    return total


def kernel(
    sizes, load_ref, kappa_ref, wet_ref, sol_out, res_out,
    other_load, other_coeff, own_coeff, load, coeffs, sol, total, inverse, cinv, face, packed, got, cgot,
    ex_send, ex_recv, k_send, k_recv, f_send, f_recv, c_send, c_recv,
):
    ex_count, ey_count, lin_count, layers, width = sizes
    ex, ey, lin = lax.axis_index("ex"), lax.axis_index("ey"), lax.axis_index("lin")
    rows = ey_count * lin_count
    row = ey * lin_count + lin
    own = REACH

    sub = lax.broadcasted_iota(jnp.int32, (2 * layers, width), 0)
    lane = lax.broadcasted_iota(jnp.int32, (2 * layers, width), 1)
    layer = sub % layers
    bottom, top = layer == 0, layer == layers - 1
    first_lane, last_lane = lane == 0, lane == width - 1
    near = jnp.where(ex == 0, lane, width - 1 - lane)
    real = (sub < layers) | (near < HALO)

    def like(mask, x):
        return jnp.broadcast_to(mask, x.shape) if x.ndim == 3 else mask

    def before(x):
        y = pltpu.roll(x, 1, x.ndim - 1)
        return jnp.where(like(first_lane, x), pltpu.roll(y, layers, x.ndim - 2), y)

    def after(x):
        y = pltpu.roll(x, width - 1, x.ndim - 1)
        return jnp.where(like(last_lane, x), pltpu.roll(y, layers, x.ndim - 2), y)

    def below(low, high):
        return jnp.where(like(bottom, low), low, low + pltpu.roll(high, 1, low.ndim - 2))

    def above(low):
        return jnp.where(like(top, low), 0.0, pltpu.roll(low, 2 * layers - 1, low.ndim - 2))

    def place(at):
        return (ex, at // lin_count, at % lin_count)

    def partners(fn):
        for d in range(1, REACH + 1):
            @pl.when(row >= d)
            def _():
                fn(row - d, own + d, own - d)

            @pl.when(row + d < rows)
            def _():
                fn(row + d, own - d, own + d)

    coeffs[...] = jnp.zeros_like(coeffs)
    cgot[...] = jnp.zeros_like(cgot)
    got[...] = jnp.zeros_like(got)
    barrier = pltpu.get_barrier_semaphore()
    pl.semaphore_signal(barrier, inc=1, device_id=(1 - ex, ey, lin), device_id_type=MESH)
    partners(lambda at, theirs, mine: pl.semaphore_signal(
        barrier, inc=1, device_id=place(at), device_id_type=MESH))

    coeff_own = kappa_ref[...] * jnp.where(wet_ref[...] == 1, F32(1.0), F32(0.05))
    own_coeff[...] = coeff_own

    pl.semaphore_wait(barrier, 1 + jnp.minimum(row, REACH) + jnp.minimum(rows - 1 - row, REACH))

    def ex_copy(src, dst, i):
        return pltpu.make_async_remote_copy(
            src_ref=src, dst_ref=dst, send_sem=ex_send.at[i], recv_sem=ex_recv.at[i],
            device_id=(1 - ex, ey, lin), device_id_type=MESH)

    coeff_copy = ex_copy(own_coeff, other_coeff, 0)
    load_copy = ex_copy(load_ref, other_load, 1)
    coeff_copy.start()
    load_copy.start()
    sol[...] = jnp.zeros_like(sol)
    coeff_copy.wait()
    coeffs[own] = jnp.where(real, jnp.concatenate([coeff_own, other_coeff[...]], axis=0), 0.0)

    def k_copy(at, theirs, mine):
        return pltpu.make_async_remote_copy(
            src_ref=coeffs.at[own], dst_ref=coeffs.at[theirs],
            send_sem=k_send.at[mine], recv_sem=k_recv.at[theirs],
            device_id=place(at), device_id_type=MESH)

    def k_wait(at, theirs, mine):
        pltpu.make_async_remote_copy(
            src_ref=coeffs.at[own], dst_ref=coeffs.at[mine],
            send_sem=k_send.at[mine], recv_sem=k_recv.at[mine],
            device_id=place(at), device_id_type=MESH).wait()

    partners(lambda *p: k_copy(*p).start())
    load_copy.wait()

    def join(i, _):
        for k in range(N * N):
            at = i * N * N + k
            load[at] = jnp.where(real, jnp.concatenate([load_ref[at], other_load[at]], axis=0), 0.0)
        return 0

    lax.fori_loop(0, N, join, 0)
    def inverted(x):
        return jnp.where(x > 0.0, 1.0 / jnp.where(x > 0.0, x, 1.0), 0.0)

    def invert():
        partners(k_wait)
        here = coeffs[own]
        for kind, x in enumerate((here, here + coeffs[own - 1], here + coeffs[own + 1])):
            xc = x + before(x)
            for slot, y in enumerate((x, xc, below(x, x), below(xc, xc))):
                inverse[kind * 4 + slot] = inverted(y)
        pairs = coeffs[0:2 * REACH] + coeffs[1:2 * REACH + 1]
        pairs = pairs + before(pairs)
        pairs = below(pairs, pairs)
        corner = 3.0 * COARSE_STIFF[0, 0] * COARSE_MASS[0, 0] ** 2
        cinv[...] = float(COARSE_RELAX / corner) * inverted(pairs)

    def plane_local(b):
        v = [[sol[node(a, b, c)] for c in range(N)] for a in range(N)]
        acc = [line_apply(v[a]) for a in range(N)]
        for c in range(N):
            column = line_apply([v[a][c] for a in range(N)])
            for a in range(N):
                acc[a][c] = acc[a][c] + column[a]
        coeff = coeffs[own]
        out = []
        for a in range(N):
            line = []
            for c in range(N):
                parts = line_parts([sol[node(a, k, c)] for k in range(N)])
                side = min(b, N - 1 - b)
                term = row_even(side, parts)
                if b < 2:
                    term = term + row_odd(side, parts)
                elif b > 2:
                    term = term - row_odd(side, parts)
                value = acc[a][c] + term
                line.append(load[node(a, b, c)] - float(W3[a, b, c]) * coeff * value)
            out.append(line)
        return out

    def gather_plane(f):
        h = []
        for a in range(N):
            h.append([f[a][0] + before(f[a][N - 1])] + f[a][1:N - 1])
        return [[below(h[0][c], h[N - 1][c]) for c in range(N - 1)]] + h[1:N - 1]

    def put_plane(b, values, ref):
        for a in range(N - 1):
            line = list(values[a])
            line.append(after(line[0]))
            for c in range(N):
                ref[node(a, b, c)] = line[c]
                if a == 0:
                    ref[node(N - 1, b, c)] = above(line[c])

    def update_plane(b, scale):
        kind = 0 if 0 < b < N - 1 else (1 if b == 0 else 2)
        values = []
        for a in range(N - 1):
            line = []
            for c in range(N - 1):
                inv = inverse[kind * 4 + (2 if a == 0 else 0) + (1 if c == 0 else 0)] * scale
                line.append(sol[node(a, b, c)] + float(FINE_RELAX / K3[a, b, c]) * inv * total[(b * 4 + a) * 4 + c])
            values.append(line)
        put_plane(b, values, sol)

    def c_copy(cycle, at, theirs, mine):
        return pltpu.make_async_remote_copy(
            src_ref=cgot.at[cycle, own], dst_ref=cgot.at[cycle, theirs],
            send_sem=c_send.at[mine], recv_sem=c_recv.at[cycle, theirs],
            device_id=place(at), device_id_type=MESH)

    def c_wait(cycle, at, theirs, mine):
        pltpu.make_async_remote_copy(
            src_ref=cgot.at[cycle, own], dst_ref=cgot.at[cycle, mine],
            send_sem=c_send.at[mine], recv_sem=c_recv.at[cycle, mine],
            device_id=place(at), device_id_type=MESH).wait()

    def gather(q, j):
        h = [q[i, j, 0] + before(q[i, j, 1]) for i in range(2)]
        return below(h[0], h[1])

    def coarse_send(cycle):
        q = {}
        for b in range(N):
            side = {0: 0, N - 1: 1}.get(b)
            f = [[total[(b * 4 + a) * 4 + c] if side is None else face[side, a * 4 + c]
                  for c in range(N - 1)] for a in range(N - 1)]
            g = [[mix((INTERP[c, k], f[a][c]) for c in range(N - 1)) for k in range(2)] for a in range(N - 1)]
            for i in range(2):
                for k in range(2):
                    h = mix((INTERP[a, i], g[a][k]) for a in range(N - 1))
                    for j in range(2):
                        if INTERP[b, j] != 0:
                            term = scaled(INTERP[b, j], h)
                            q[i, j, k] = q[i, j, k] + term if (i, j, k) in q else term
        for j in range(2):
            cgot[cycle, own, j] = gather(q, j)
        partners(lambda *p: c_copy(cycle, *p).start())

    def correct(cycle):
        partners(lambda *p: c_wait(cycle, *p))
        lines = 2 * REACH
        rc = cgot[cycle, 0:lines, 1] + cgot[cycle, 1:lines + 1, 0]
        inv = cinv[...]
        correction = inv * rc
        coeff = coeffs[1:lines]

        def corners(x):
            right = after(x)
            return {(0, 0): x, (0, 1): right, (1, 0): above(x), (1, 1): above(right)}

        def two(m, x, y):
            return [mix(((m[p, 0], x), (m[p, 1], y))) for p in range(2)]

        for sweep in range(NC - 1):
            nodes = corners(correction)
            v = {(i, j, k): nodes[i, k][j:j + lines - 1] for i in range(2) for j in range(2) for k in range(2)}

            def along(m, v, axis):
                out = {}
                for x in range(2):
                    for y in range(2):
                        key = [(0, x, y), (x, 0, y), (x, y, 0)][axis]
                        key1 = [(1, x, y), (x, 1, y), (x, y, 1)][axis]
                        out[key], out[key1] = two(m, v[key], v[key1])
                return out

            mc = along(COARSE_MASS, v, 2)
            first = along(COARSE_STIFF, along(COARSE_MASS, mc, 1), 0)
            rest = along(COARSE_STIFF, mc, 1)
            third = along(COARSE_MASS, along(COARSE_STIFF, v, 2), 1)
            rest = along(COARSE_MASS, {key: rest[key] + third[key] for key in rest}, 0)
            q2 = {key: coeff * (first[key] + rest[key]) for key in rest}
            low, high = gather(q2, 0), gather(q2, 1)
            zero = jnp.zeros_like(low[0:1])
            image = jnp.concatenate([low, zero], axis=0) + jnp.concatenate([zero, high], axis=0)
            correction = correction + inv * (rc - image)
        ends = [corners(correction[own - 2 + m]) for m in range(4)]

        def interpolated(k, b):
            return {key: mix(((INTERP[b, j], ends[k + j][key]) for j in range(2))) for key in ends[0]}

        def operated(k, b):
            coeff = coeffs[own - 1 + k]
            half = {key: (0.5 * coeff) * value for key, value in interpolated(k, b).items()}
            f = [[None] * N for _ in range(N)]

            def put(a, c, value):
                f[a][c] = value if f[a][c] is None else f[a][c] + value

            rise_c = [half[i, 1] - half[i, 0] for i in range(2)]
            rise_a = [half[1, i] - half[0, i] for i in range(2)]
            for n in range(N):
                value = float(WEIGHTS[n] * WEIGHTS[b]) * mix(((INTERP[n, i], rise_c[i]) for i in range(2)))
                put(n, 0, value)
                put(n, N - 1, -value)
                value = float(WEIGHTS[n] * WEIGHTS[b]) * mix(((INTERP[n, i], rise_a[i]) for i in range(2)))
                put(0, n, value)
                put(N - 1, n, -value)
            if b in (0, N - 1):
                sign = 0.5 if b == 0 else -0.5
                rise_b = {key: (sign * coeff) * (ends[k + 1][key] - ends[k][key]) for key in ends[0]}
                for a in range(N):
                    pair = [mix(((INTERP[a, i], rise_b[i, x]) for i in range(2))) for x in range(2)]
                    for c in range(N):
                        put(a, c, float(WEIGHTS[a] * WEIGHTS[c]) * mix(((INTERP[c, x], pair[x]) for x in range(2))))
            return f

        for b in range(N):
            sums = [gather_plane(operated(1, b))]
            if b == 0:
                sums.append(gather_plane(operated(0, N - 1)))
            if b == N - 1:
                sums.append(gather_plane(operated(2, 0)))
            mid = interpolated(1, b)
            for a in range(N - 1):
                pair = [mix(((INTERP[a, i], mid[i, k]) for i in range(2))) for k in range(2)]
                for c in range(N - 1):
                    at = node(a, b, c)
                    sol[at] = sol[at] + mix(((INTERP[c, k], pair[k]) for k in range(2)))
                    if sums[0][a][c] is not None:
                        at = (b * 4 + a) * 4 + c
                        value = total[at]
                        for one in sums:
                            value = value + one[a][c]
                        total[at] = value

    fold = width // HALO
    block = lax.rem(lane + jnp.where(ex == 0, 0, HALO - 1), width) // HALO
    lower = sub < layers

    def swap(x):
        return pltpu.roll(x, layers, 0)

    def pack(side, x):
        for p in range(8):
            packed[side, p] = jnp.where(lower, x[2 * p], swap(x[2 * p + 1]))
        for p in range(8 // fold):
            halves = []
            for h in range(2):
                group = x[(2 * p + h) * fold:(2 * p + h + 1) * fold]
                mixed = group[0]
                for j in range(1, fold):
                    mixed = jnp.where(block == j, pltpu.roll(group[j], HALO * j, 1), mixed)
                halves.append(mixed)
            packed[side, 8 + p] = jnp.where(lower, swap(halves[0]), halves[1])

    def unpack(slot, side):
        x = []
        for p in range(8 // fold):
            tile = got[slot, side, 8 + p]
            for half in (swap(tile), tile):
                for j in range(fold):
                    other = half if j == 0 else pltpu.roll(half, width - HALO * j, 1)
                    n = len(x)
                    mine = got[slot, side, n // 2]
                    mine = mine if n % 2 == 0 else swap(mine)
                    x.append(jnp.where(lower, mine, jnp.where(block == 0, other, 0.0)))
        return x

    def face_copy(slot, side, at):
        return pltpu.make_async_remote_copy(
            src_ref=packed.at[side], dst_ref=got.at[slot, 1 - side],
            send_sem=f_send.at[side], recv_sem=f_recv.at[slot, 1 - side],
            device_id=place(at), device_id_type=MESH)

    def face_wait(slot, side, at):
        pltpu.make_async_remote_copy(
            src_ref=packed.at[side], dst_ref=got.at[slot, side],
            send_sem=f_send.at[side], recv_sem=f_recv.at[slot, side],
            device_id=place(at), device_id_type=MESH).wait()

    def both(fn):
        @pl.when(row >= 1)
        def _():
            fn(0, row - 1)

        @pl.when(row + 1 < rows)
        def _():
            fn(1, row + 1)

    def step(s, _):
        slot = lax.rem(s, 2)

        cycle = s // (NPRE + NPOST)
        coarse = (lax.rem(s, NPRE + NPOST) == NPRE) & (s < STEPS - 1)

        for side in range(2):
            summed = gather_plane(plane_local(side * (N - 1)))
            for a in range(N - 1):
                for c in range(N - 1):
                    face[side, a * 4 + c] = summed[a][c]
            pack(side, [value for values in summed for value in values])
        both(lambda side, at: face_copy(slot, side, at).start())
        for b in range(1, N - 1):
            summed = gather_plane(plane_local(b))
            for a in range(N - 1):
                for c in range(N - 1):
                    total[(b * 4 + a) * 4 + c] = summed[a][c]
        scale = jnp.where(s < STEPS - 1, F32(1.0), F32(0.0))

        @pl.when(s == 0)
        def _():
            invert()

        @pl.when(coarse)
        def _():
            coarse_send(cycle)

        @pl.when(jnp.logical_not(coarse))
        def _():
            for b in range(1, N - 1):
                update_plane(b, scale)

        both(lambda side, at: face_wait(slot, side, at))
        for side in range(2):
            theirs = unpack(slot, side)
            for i in range(16):
                total[side * (N - 1) * 16 + i] = face[side, i] + theirs[i]

        @pl.when(coarse)
        def _():
            correct(cycle)
            for b in range(1, N - 1):
                update_plane(b, scale)

        for side in range(2):
            update_plane(side * (N - 1), scale)
        return 0

    lax.fori_loop(0, STEPS, step, 0)

    for b in range(N):
        put_plane(b, [[total[(b * 4 + a) * 4 + c] for c in range(N - 1)] for a in range(N - 1)], load)

    def out(i, _):
        for k in range(N * N):
            at = i * N * N + k
            sol_out[at] = sol[at][0:layers]
            res_out[at] = load[at][0:layers]
        return 0

    lax.fori_loop(0, N, out, 0)


def per_device(sizes, load, kappa, wet):
    layers, _, width = kappa.shape
    nodes = N * N * N
    tile = (2 * layers, width)
    sizes = sizes + (layers, width)
    out = jax.ShapeDtypeStruct((nodes, layers, width), F32)
    vmem = pl.BlockSpec(memory_space=pltpu.VMEM)
    span = 2 * REACH + 1
    messages = 8 + 8 * HALO // width
    dma = pltpu.SemaphoreType.DMA
    solution, residual = pl.pallas_call(
        functools.partial(kernel, sizes),
        out_shape=(out, out),
        in_specs=[vmem] * 3,
        out_specs=(vmem, vmem),
        scratch_shapes=[
            pltpu.VMEM((nodes, layers, width), F32),
            pltpu.VMEM((layers, width), F32),
            pltpu.VMEM((layers, width), F32),
            pltpu.VMEM((nodes,) + tile, F32),
            pltpu.VMEM((span,) + tile, F32),
            pltpu.VMEM((nodes,) + tile, F32),
            pltpu.VMEM((N * 16,) + tile, F32),
            pltpu.VMEM((12,) + tile, F32),
            pltpu.VMEM((2 * REACH,) + tile, F32),
            pltpu.VMEM((2, 16) + tile, F32),
            pltpu.VMEM((2, messages) + tile, F32),
            pltpu.VMEM((2, 2, messages) + tile, F32),
            pltpu.VMEM((CYCLES, span, 2) + tile, F32),
            dma((2,)), dma((2,)), dma((span,)), dma((span,)),
            dma((2,)), dma((2, 2)), dma((span,)), dma((CYCLES, span)),
        ],
        compiler_params=pltpu.CompilerParams(collective_id=0, has_side_effects=True),
    )(load.reshape(nodes, layers, width), kappa.reshape(layers, width), wet.reshape(layers, width))
    return solution.reshape(load.shape), residual.reshape(load.shape)


def solution(mesh):
    sizes = tuple(mesh.shape[name] for name in ("ex", "ey", "lin"))
    field = P(None, None, None, None, ("ey", "lin"), "ex")
    cell = P(None, ("ey", "lin"), "ex")
    return jax.shard_map(
        functools.partial(per_device, sizes), mesh=mesh, in_specs=(field, cell, cell),
        out_specs=(field, field), check_vma=False,
    )
```

profile of v0, /device:TPU:4, one launch (start us, length us, event | category | flops | bytes accessed | tf_op | source)
XLA Modules:
  0.0 57.8 jit_solution(12819081522678891903)
XLA Ops:
  0.6 54.7 %shard_map.50 = (f32[125,4,128]{2,1,0:T(4,128)}, f32[125,4,128]{2,1,0:T(4,128)}) custom-call(f32[125,4,128]{2,1,0:T(4,128)} %bitcast.9, f32[4,128]{1,0:T(4,128)} %bitcast.12, s32[4,128]{1,0:T(4,128)} %bitcast.13), custom_call_target="tpu_custom_call" | custom-call | tf_op jit(solution)/shard_map/pallas_call | solution.py:501
  55.4 0.0 copy-start
  55.4 1.7 %copy.9 = f32[5,5,5,4,1,128]{5,4,3,2,1,0:T(1,128)} copy(f32[5,5,5,4,1,128]{5,4,3,2,1,0:T(1,128)} %bitcast.11) | data formatting | bytes 512000
  57.1 0.0 copy-done
  57.1 0.7 %copy.10 = f32[5,5,5,4,1,128]{5,4,3,2,1,0:T(1,128)} copy(f32[5,5,5,4,1,128]{5,4,3,2,1,0:T(1,128)S(1)} %bitcast.10) | data formatting | bytes 512000
Async XLA Ops:
  55.4 1.7 %copy-start = (f32[125,4,128]{2,1,0:T(4,128)S(1)}, f32[125,4,128]{2,1,0:T(4,128)}, u32[]{:S(2)}) copy-start(f32[125,4,128]{2,1,0:T(4,128)} %get-tuple-element.5) | copy-start | bytes 768004
where the time goes:
time: 58 us; the launch traced here: 57.8 us
  Pallas kernels  54.7 us (94%)
  local copies, waits for them, and re-layouts  2.41 us (4%)
  between operations  0.65 us (1%)
    pallas_call x1, Pallas kernels, per_device(): pl.pallas_call(functools.partial(kernel, sizes), out_shape=(out, out), in...  54.7 us
    unnamed x4, local copies, waits for them, and re-layouts  2.41 us

commit v1 on v0

v1 whole, which is shorter than its diff:
```python
import functools
import math

import jax
import jax.numpy as jnp
import numpy as np
from jax import lax
from jax.experimental import pallas as pl
from jax.experimental.pallas import tpu as pltpu
from jax.sharding import PartitionSpec as P

N = 5
CYCLES = 2
NPRE = 2
NPOST = 2
NC = 4
PERIOD = NPRE + NPOST
FINE_RELAX = 0.25
COARSE_RELAX = 0.4
STEPS = CYCLES * PERIOD + 1
REACH = NC + 2
SPAN = 2 * REACH
OWN = REACH
HALO = 32
MESH = pl.DeviceIdType.MESH
F32 = jnp.float32


def node_tables():
    points = np.array([-1.0, -math.sqrt(3.0 / 7.0), 0.0, math.sqrt(3.0 / 7.0), 1.0])
    weights = np.array([0.1, 49.0 / 90.0, 32.0 / 45.0, 49.0 / 90.0, 0.1])
    eye_table = np.eye(points.shape[0])
    spread = points[:, None] - points[None, :] + eye_table
    factors = np.prod(spread, axis=1)
    deriv = factors[:, None] / (factors[None, :] * spread)
    deriv = np.where(eye_table > 0, (np.sum(1.0 / spread, axis=1) - 1.0)[:, None], deriv)
    stiff = deriv.T @ (weights[:, None] * deriv)
    mass = eye_table * weights[:, None]
    interp = np.stack([(1.0 - points) / 2.0, (1.0 + points) / 2.0], axis=1)
    return stiff, weights, interp, interp.T @ stiff @ interp, interp.T @ mass @ interp


S, WEIGHTS, INTERP, SC, WC = node_tables()
ALPHA = (S[0, 0] + S[0, 4]) / 2
BETA = (S[0, 1] + S[0, 3]) / 2
GAMMA = (S[1, 1] + S[1, 3]) / 2
KAPPA = (S[0, 1] - S[0, 3]) / (S[0, 0] - S[0, 4])
ODD = (S[0, 0] - S[0, 4]) / 2
DELTA = (S[1, 1] - S[1, 3]) / (2 * KAPPA ** 2) - ODD
W0, W1, W2 = WEIGHTS[:3]
MU = [W0 / 2, W1 / 2, W2 / 4, W1 / (2 * KAPPA ** 2), W0 / 2]
MUB = [W0, W1 / 2, W2 / 4, W1 / (2 * KAPPA ** 2), W0]
NU = [1.0, 2.0, 4.0, 2 * KAPPA ** 2, 1.0]
SLOPE = KAPPA * (INTERP[1, 0] - INTERP[3, 0])
RISE = ODD * (1 + SLOPE)
NODE = [0, 1, 2, 1, 4]
DIAG = np.diag(S) / WEIGHTS
W3 = WEIGHTS[:, None, None] * WEIGHTS[None, :, None] * WEIGHTS[None, None, :]
K3 = W3 * (DIAG[:, None, None] + DIAG[None, :, None] + DIAG[None, None, :])
CS = (SC[0, 0] - SC[0, 1]) / 2
CE, CO = (WC[0, 0] + WC[0, 1]) / 2, (WC[0, 0] - WC[0, 1]) / 2
C1, C2, C3 = CS * CE * CE, 2 * CS * CO * CE, 3 * CS * CO * CO
SENDS = [d for d in range(-REACH + 1, REACH + 1) if d != 0]
RECVS = [d for d in range(-REACH, REACH) if d != 0]


def st(b, a, c):
    return (b * 4 + a) * 4 + c


def xi(b, i, k):
    return (b * N + i) * N + k


def line_apply(e0, e1, z, o1, o0, scale):
    q0, q1 = e0 - z, e1 - z
    r0 = float(ALPHA * scale) * q0 + float(BETA * scale) * q1
    r1 = float(BETA * scale) * q0 + float(GAMMA * scale) * q1
    s0 = float(ODD * scale) * (o0 + o1)
    return r0, r1, r0 + r1, s0 + float(DELTA * scale) * o1, s0


def plus(x, y):
    if x is None or y is None:
        return x if y is None else y
    return x + y


def minus(x, y):
    if y is None:
        return x
    return -y if x is None else x - y


def kernel(
    sizes, load_ref, kappa_ref, wet_ref, sol_out, res_out,
    ghost_load, halo_pack, halo_got, own_coeff, other_coeff, coeffs,
    rhs, sol, tot, sinv, xs, bs, face, packed, got, cgot, cinv,
    ex_send, ex_recv, k_send, k_recv, f_send, f_recv, c_send, c_recv,
):
    ex_count, ey_count, lin_count, layers, width = sizes
    ex, ey, lin = lax.axis_index("ex"), lax.axis_index("ey"), lax.axis_index("lin")
    rows = ey_count * lin_count
    row = ey * lin_count + lin
    par = lax.rem(lin, 2)
    sgn = 1 - 2 * par
    fold = width // HALO
    groups = -(-N * N // fold)

    sub = lax.broadcasted_iota(jnp.int32, (2 * layers, width), 0)
    lane = lax.broadcasted_iota(jnp.int32, (2 * layers, width), 1)
    layer = sub % layers
    bottom, top = layer == 0, layer == layers - 1
    first_lane, last_lane = lane == 0, lane == width - 1
    near = jnp.where(ex == 0, lane, width - 1 - lane)
    real = (sub < layers) | (near < HALO)
    lower = sub < layers

    def before(x):
        y = pltpu.roll(x, 1, 1)
        return jnp.where(first_lane, pltpu.roll(y, layers, 0), y)

    def after(x):
        y = pltpu.roll(x, width - 1, 1)
        return jnp.where(last_lane, pltpu.roll(y, layers, 0), y)

    def below(low, high):
        return jnp.where(bottom, low, low + pltpu.roll(high, 1, 0))

    def above(low):
        return jnp.where(top, 0.0, pltpu.roll(low, 2 * layers - 1, 0))

    def there(d):
        at = row + sgn * d
        return (at >= 0) & (at < rows)

    def place(d, other=False):
        at = row + sgn * d
        return (1 - ex if other else ex, at // lin_count, at % lin_count)

    def when_there(d, fn):
        @pl.when(there(d))
        def _():
            fn(d)

    def slot_at(d):
        return REACH + (-d if d % 2 == 0 else d)

    def remote(src, dst, send, recv, device):
        return pltpu.make_async_remote_copy(
            src_ref=src, dst_ref=dst, send_sem=send, recv_sem=recv, device_id=device, device_id_type=MESH)

    coeffs[...] = jnp.zeros_like(coeffs)
    cgot[...] = jnp.zeros_like(cgot)

    @pl.when(jnp.logical_not(there(-1)))
    def _():
        ghost_load[...] = jnp.zeros_like(ghost_load)
        halo_got[1] = jnp.zeros_like(halo_got[1])

    def greet(device):
        pl.semaphore_signal(pltpu.get_barrier_semaphore(), inc=1, device_id=device, device_id_type=MESH)

    greet((1 - ex, ey, lin))
    when_there(-1, lambda d: greet(place(d, True)))
    expected = 1 + there(-1).astype(jnp.int32)
    for d in range(1, REACH + 1):
        for e in (-d, d):
            when_there(e, lambda e: greet(place(e)))
            expected = expected + there(e).astype(jnp.int32)

    coeff_own = kappa_ref[...] * jnp.where(wet_ref[...] == 1, F32(1.0), F32(0.05))
    own_coeff[...] = coeff_own

    def raw(a, b, c):
        return (a * N + b + par * (N - 1 - 2 * b)) * N + c

    half_lane = lax.broadcasted_iota(jnp.int32, (layers, width), 1)
    source = jnp.where(ex == 0, fold - 1, 0)
    turn = (half_lane // HALO + fold - source) % fold

    def pack_plane(b, _):
        for g in range(groups):
            mixed = None
            for j in range(fold):
                n = g * fold + j
                if n < N * N:
                    x = load_ref[raw(n // N, b, n % N)]
                    mixed = x if j == 0 else jnp.where(turn == j, pltpu.roll(x, HALO * j, 1), mixed)
            halo_pack[b * groups + g] = mixed
        return 0

    lax.fori_loop(0, N, pack_plane, 0)
    pl.semaphore_wait(pltpu.get_barrier_semaphore(), expected)

    across = (1 - ex, ey, lin)
    coeff_copy = remote(own_coeff, other_coeff, ex_send.at[0], ex_recv.at[0], across)
    halo_copy = remote(halo_pack, halo_got.at[0], ex_send.at[1], ex_recv.at[1], across)

    def load_copy():
        return remote(load_ref, ghost_load, ex_send.at[2], ex_recv.at[2], place(-1))

    def corner_copy():
        return remote(halo_pack, halo_got.at[1], ex_send.at[3], ex_recv.at[3], place(-1, True))

    coeff_copy.start()
    halo_copy.start()
    when_there(-1, lambda d: load_copy().start())
    when_there(-1, lambda d: corner_copy().start())

    coeff_copy.wait()
    coeffs[OWN] = jnp.where(real, jnp.concatenate([coeff_own, other_coeff[...]], axis=0), 0.0)
    for d in SENDS:
        when_there(d, lambda d: remote(
            coeffs.at[OWN], coeffs.at[slot_at(d)], k_send.at[REACH + d], k_recv.at[slot_at(d)], place(d)).start())

    def to_dual(f):
        return [(f[1] + f[3]) * 0.5, f[2] * 0.5, (f[1] - f[3]) * float(0.5 / KAPPA)]

    def load_plane(r, b, own_ref):
        source_b = b if r == 0 else N - 1 - b
        tiles = []
        for n in range(N * N):
            mine = own_ref[raw(n // N, b, n % N)]
            other = halo_got[r, source_b * groups + n // fold]
            j = n % fold
            if j:
                other = pltpu.roll(other, width - HALO * j, 1)
            tiles.append(jnp.where(real, jnp.concatenate([mine, other], axis=0), 0.0))
        lines = []
        for a in range(N):
            f = tiles[a * N:a * N + N]
            lines.append([f[0] + before(f[4])] + to_dual(f))
        columns = []
        for c in range(4):
            f = [lines[a][c] for a in range(N)]
            columns.append([below(f[0], f[4])] + to_dual(f))
        return [[columns[c][a] for c in range(4)] for a in range(4)]

    def build_rhs(r, own_ref):
        for b, at in ((0, 0), (4, 4), (2, 2), (1, 1), (3, 3)):
            p = load_plane(r, b, own_ref)
            for a in range(4):
                for c in range(4):
                    x = p[a][c]
                    if b == 2:
                        x = x * 0.5
                    if b == 3:
                        first = rhs[r, st(1, a, c)]
                        rhs[r, st(3, a, c)] = (first - x) * float(0.5 / KAPPA)
                        rhs[r, st(1, a, c)] = (first + x) * 0.5
                    else:
                        rhs[r, st(at, a, c)] = x

    halo_copy.wait()
    build_rhs(0, load_ref)

    block = lax.rem(lane + jnp.where(ex == 0, 0, HALO - 1), width) // HALO

    def swap(x):
        return pltpu.roll(x, layers, 0)

    def pack(s, x):
        for p in range(8):
            packed[s, p] = jnp.where(lower, x[2 * p], swap(x[2 * p + 1]))
        for p in range(8 // fold):
            halves = []
            for h in range(2):
                group = x[(2 * p + h) * fold:(2 * p + h + 1) * fold]
                mixed = group[0]
                for j in range(1, fold):
                    mixed = jnp.where(block == j, pltpu.roll(group[j], HALO * j, 1), mixed)
                halves.append(mixed)
            packed[s, 8 + p] = jnp.where(lower, swap(halves[0]), halves[1])

    def unpack(kind, s):
        x = []
        for p in range(8 // fold):
            tile = got[kind, s, 8 + p]
            for half in (swap(tile), tile):
                for j in range(fold):
                    other = half if j == 0 else pltpu.roll(half, width - HALO * j, 1)
                    n = len(x)
                    mine = got[kind, s, n // 2]
                    mine = mine if n % 2 == 0 else swap(mine)
                    x.append(jnp.where(lower, mine, jnp.where(block == 0, other, 0.0)))
        return x

    def near_copy(s):
        return remote(packed.at[s], got.at[0, s], f_send.at[0, s], f_recv.at[0, s], place(1))

    def far_copy(s):
        return remote(packed.at[s], got.at[1, s], f_send.at[1, s], f_recv.at[1, s], place(2))

    def send_face(s, values):
        pack(s, values)
        near_copy(s).start()

        @pl.when(there(2) & (s < STEPS - 1))
        def _():
            far_copy(s).start()

    def add_near(s):
        near_copy(s).wait()
        for n, x in enumerate(unpack(0, s)):
            tot[0, 64 + n] = tot[0, 64 + n] + x

    def add_far(s):
        @pl.when(there(-2))
        def _():
            far_copy(s).wait_recv()
            for n, x in enumerate(unpack(1, s)):
                tot[1, n] = tot[1, n] + x

    def expand(r):
        for b in range(N):
            w = []
            for a in range(4):
                v = [sol[r, st(b, a, c)] for c in range(4)]
                up = after(v[0])
                w.append([v[0] + up, v[1], v[2], v[3], v[0] - up])
            for k in range(N):
                up = above(w[0][k])
                xs[r, xi(b, 0, k)] = w[0][k] + up
                xs[r, xi(b, 4, k)] = w[0][k] - up
                for a in range(1, 4):
                    xs[r, xi(b, a, k)] = w[a][k]

    def cross(r):
        for i in range(N):
            for k in range(N):
                v = [xs[r, xi(b, i, k)] for b in range(N)]
                r0, r1, rz, s1, s0 = line_apply(v[0] + v[4], v[1], v[2], v[3], v[0] - v[4], MU[i] * MU[k])
                for b, x in enumerate((r0 + s0, r1, rz, s1, r0 - s0)):
                    bs[r, xi(b, i, k)] = x

    def gather(y):
        g = []
        for k in range(N):
            low, high = plus(y[0][k], y[4][k]), minus(y[0][k], y[4][k])
            g.append([None if low is None else below(low, high)] + [y[i][k] for i in range(1, 4)])
        h = []
        for a in range(4):
            low, high = plus(g[0][a], g[4][a]), minus(g[0][a], g[4][a])
            h.append([None if low is None else low + before(high)] + [g[k][a] for k in range(1, 4)])
        return h

    def plane(r, b):
        coeff = coeffs[OWN - r]
        x = [[xs[r, xi(b, i, k)] for k in range(N)] for i in range(N)]
        along_c = [line_apply(*x[i], MUB[b] * MU[i]) for i in range(N)]
        along_a = [line_apply(*[x[i][k] for i in range(N)], MUB[b] * MU[k]) for k in range(N)]
        y = []
        for i in range(N):
            line = []
            for k in range(N):
                terms = sorted(((b == 2, bs[r, xi(b, i, k)]), (k == 2, along_c[i][k]), (i == 2, along_a[k][i])),
                               key=lambda t: t[0])
                total = -terms[0][1] if terms[0][0] else terms[0][1]
                for negative, term in terms[1:]:
                    total = total - term if negative else total + term
                line.append(coeff * total)
            y.append(line)
        h = gather(y)
        return [rhs[r, st(b, a, c)] - h[a][c] for a in range(4) for c in range(4)]

    def put(r, b, values):
        for n, x in enumerate(values):
            tot[r, b * 16 + n] = x

    def update(r, b):
        for n in range(b * 16, b * 16 + 16):
            sol[r, n] = sol[r, n] + sinv[r, n] * tot[r, n]

    def inverted(x):
        return jnp.where(x > 0.0, 1.0 / jnp.where(x > 0.0, x, 1.0), 0.0)

    def invert():
        for r in range(2):
            here = coeffs[OWN - r]
            for bl, x in (((1, 2, 3), here), ((0,), here + coeffs[OWN - r - 1]), ((4,), here + coeffs[OWN - r + 1])):
                xc = x + before(x)
                tiles = [[inverted(below(xc, xc)), inverted(below(x, x))], [inverted(xc), inverted(x)]]
                for b in bl:
                    for a in range(4):
                        for c in range(4):
                            factor = FINE_RELAX * NU[a] * NU[b] * NU[c] / K3[NODE[a], NODE[b], NODE[c]]
                            sinv[r, st(b, a, c)] = float(factor) * tiles[min(a, 1)][min(c, 1)]
        corner = 3.0 * SC[0, 0] * WC[0, 0] ** 2
        for i in range(SPAN - 1):
            pair = coeffs[i] + coeffs[i + 1]
            pair = pair + before(pair)
            cinv[i] = float(COARSE_RELAX / corner) * inverted(below(pair, pair))

    def halves(v):
        even, odd = v[1] + v[2], float(SLOPE) * v[3]
        return even + odd, even - odd

    def coarse_send(cycle):
        q = [[], []]
        for n in range(16):
            v = [face[0, n], tot[0, 16 + n], tot[0, 32 + n], tot[0, 48 + n]]
            low, high = halves(v)
            q[0].append(v[0] + low)
            q[1].append(face[1, n] + high)
        for j in range(2):
            lines = []
            for a in range(4):
                v = q[j][a * 4:a * 4 + 4]
                low, high = halves(v)
                lines.append((v[0] + low) + before(high))
            low, high = halves(lines)
            cgot[cycle, OWN, j] = below(lines[0] + low, high)
        for d in SENDS:
            when_there(d, lambda d: remote(
                cgot.at[cycle, OWN], cgot.at[cycle, slot_at(d)], c_send.at[REACH + d], c_recv.at[cycle, slot_at(d)],
                place(d)).start())

    def correct(cycle):
        for d in SENDS:
            when_there(d, lambda d: remote(
                cgot.at[cycle, OWN], cgot.at[cycle, OWN], c_send.at[REACH + d], c_recv.at[cycle, OWN],
                place(d)).wait_send())
        for d in RECVS:
            when_there(d, lambda d: remote(
                cgot.at[cycle, OWN], cgot.at[cycle, REACH + d], c_send.at[OWN], c_recv.at[cycle, REACH + d],
                place(d)).wait_recv())

        def q(e, j):
            return cgot[cycle, e, j if (e - OWN) % 2 == 0 else 1 - j]

        lines = SPAN - 1
        rc = [q(i, 1) + q(i + 1, 0) for i in range(lines)]
        x = [cinv[i] * rc[i] for i in range(lines)]

        def modes(v):
            up = after(v)
            parts = []
            for k in (v + up, v - up):
                high = above(k)
                parts.append((k + high, k - high))
            return [[parts[k][i] for k in range(2)] for i in range(2)]

        first, last = 0, lines - 1
        for sweep in range(NC - 1):
            m = {i: modes(x[i]) for i in range(first, last + 1)}
            sides = {}
            for e in range(first + 1, last + 1):
                coeff = coeffs[e]
                factor = [float(C1) * coeff, float(C2) * coeff, float(C3) * coeff]
                low, high = m[e - 1], m[e]
                part = []
                for i in range(2):
                    pair = []
                    for k in range(2):
                        odd = factor[i + k] * (low[i][k] - high[i][k])
                        if i + k == 0:
                            pair.append((odd, -odd))
                        else:
                            even = factor[i + k - 1] * (low[i][k] + high[i][k])
                            pair.append((even + odd, even - odd))
                    part.append(pair)
                sides[e] = part
            first, last = first + 1, last - 1
            new = list(x)
            for i in range(first, last + 1):
                y = [[sides[i + 1][a][k][0] + sides[i][a][k][1] for k in range(2)] for a in range(2)]
                g = [below(y[0][k] + y[1][k], y[0][k] - y[1][k]) for k in range(2)]
                image = (g[0] + g[1]) + before(g[0] - g[1])
                new[i] = x[i] + cinv[i] * (rc[i] - image)
            x = new

        base = OWN - 3
        m = {i: modes(x[i]) for i in range(base, base + 5)}
        kind = [0, 0, 0, 1, 1]
        grow = [1.0, 1.0, 1.0, SLOPE, 1.0]

        def ends(centre, weight, tilt):
            y = [[None] * N for _ in range(N)]
            for i in range(N):
                for k in range(N):
                    value = None
                    if centre is not None:
                        value = float(MU[i] * MU[k] * grow[i] * grow[k]) * centre[kind[i]][kind[k]]
                    if i == 4:
                        value = plus(value, float(RISE * weight * MU[k] * grow[k]) * tilt[1][kind[k]])
                    if k == 4:
                        value = plus(value, float(RISE * weight * MU[i] * grow[i]) * tilt[kind[i]][1])
                    y[i][k] = value
            return gather(y)

        def face_image(i):
            up, down = coeffs[i + 1], coeffs[i]
            both = up + down
            centre = [[float(RISE) * (up * (m[i][a][k] - m[i + 1][a][k]) - down * (m[i - 1][a][k] - m[i][a][k]))
                       for k in range(2)] for a in range(2)]
            tilt = [[None if a + k == 0 else both * m[i][a][k] for k in range(2)] for a in range(2)]
            h = ends(centre, W0, tilt)
            return [h[a][c] for a in range(4) for c in range(4)]

        for i, targets in ((OWN - 2, ((1, 0),)), (OWN - 1, ((1, 64), (0, 0))), (OWN, ((0, 64),))):
            values = face_image(i)
            for r, at in targets:
                for n, value in enumerate(values):
                    tot[r, at + n] = tot[r, at + n] - value
        scale = [1.0, 1.0, 1.0, SLOPE]

        def nodal(i):
            v = x[i]
            up = after(v)
            high = above(v)
            tiles = [[v, v + up, v - up], [v + high, m[i][0][0], m[i][0][1]], [v - high, m[i][1][0], m[i][1][1]]]
            pick = [0, 1, 1, 2]
            made = {}
            out = []
            for a in range(4):
                for c in range(4):
                    key = (pick[a], pick[c])
                    if key not in made:
                        factor = float(scale[a] * scale[c])
                        made[key] = tiles[key[0]][key[1]] if factor == 1.0 else factor * tiles[key[0]][key[1]]
                    out.append((key, made[key]))
            return out

        at_line = {i: nodal(i) for i in (OWN - 2, OWN - 1, OWN)}
        for r in range(2):
            low, high = OWN - 1 - r, OWN - r
            coeff = coeffs[OWN - r]
            for kindb in range(2):
                diff = [[None if a + k == 0 else
                         coeff * (m[low][a][k] - m[high][a][k] if kindb else m[low][a][k] + m[high][a][k])
                         for k in range(2)] for a in range(2)]
                h = ends(None, 1.0, diff)
                for b in ((3,) if kindb else (1, 2)):
                    factor = float(MUB[b] * (SLOPE if kindb else 1.0))
                    for a in range(4):
                        for c in range(4):
                            if h[a][c] is not None:
                                tot[r, st(b, a, c)] = tot[r, st(b, a, c)] - factor * h[a][c]
                made = {}
                for n in range(16):
                    key, lower_value = at_line[low][n]
                    upper_value = at_line[high][n][1]
                    if key not in made:
                        made[key] = (float(SLOPE) * (lower_value - upper_value) if kindb
                                     else lower_value + upper_value)
                    for b in ((3,) if kindb else (1, 2)):
                        sol[r, b * 16 + n] = sol[r, b * 16 + n] + made[key]
            for n in range(16):
                sol[r, n] = sol[r, n] + at_line[low][n][1]
                sol[r, 64 + n] = sol[r, 64 + n] + at_line[high][n][1]

    def emit(field, out_ref, dual):
        def split(mid, double, odd):
            if dual:
                odd = float(KAPPA) * odd
                return mid + odd, 2.0 * double, mid - odd
            even, odd = 0.5 * mid, float(0.5 / KAPPA) * odd
            return even + odd, 0.5 * double, even - odd

        def one(b, values):
            lines = []
            for a in range(4):
                v = values[a * 4:a * 4 + 4]
                lines.append([v[0], *split(*v[1:]), after(v[0])])
            for c in range(N):
                v = [lines[a][c] for a in range(4)]
                for a, tile in enumerate([v[0], *split(*v[1:]), above(v[0])]):
                    out_ref[raw(a, b, c)] = tile[0:layers]

        for b in (0, 4):
            one(b, [field[0, b * 16 + n] for n in range(16)])
        mids = [split(field[0, 16 + n], field[0, 32 + n], field[0, 48 + n]) for n in range(16)]
        for b in range(1, 4):
            one(b, [v[b - 1] for v in mids])

    for b in range(N):
        put(0, b, [rhs[0, b * 16 + n] for n in range(16)])
    send_face(0, [tot[0, 64 + n] for n in range(16)])
    sol[...] = jnp.zeros_like(sol)
    for d in SENDS:
        when_there(d, lambda d: remote(
            coeffs.at[OWN], coeffs.at[OWN], k_send.at[REACH + d], k_recv.at[OWN], place(d)).wait_send())
    for d in RECVS:
        when_there(d, lambda d: remote(
            coeffs.at[OWN], coeffs.at[REACH + d], k_send.at[OWN], k_recv.at[REACH + d], place(d)).wait_recv())
    invert()
    when_there(-1, lambda d: load_copy().wait())
    when_there(-1, lambda d: corner_copy().wait())
    build_rhs(1, ghost_load)
    for b in range(N):
        put(1, b, [rhs[1, b * 16 + n] for n in range(16)])
    for n in range(16):
        joined = tot[0, n] + tot[1, 64 + n]
        tot[0, n] = joined
        tot[1, 64 + n] = joined
    for b in range(4):
        update(0, b)
        update(1, b + 1)
    add_near(0)
    update(0, 4)

    def step(s, _):
        cycle = s // PERIOD
        live = s < STEPS - 1
        coarse = (lax.rem(s, PERIOD) == NPRE) & live
        deferred = lax.rem(s - 1, PERIOD) != NPRE

        expand(0)
        cross(0)
        mine = plane(0, 4)
        for n in range(16):
            face[1, n] = mine[n]
        put(0, 4, mine)
        send_face(s, mine)

        @pl.when(there(2))
        def _():
            far_copy(s - 1).wait_send()

        @pl.when(deferred)
        def _():
            add_far(s - 1)
            update(1, 0)

        expand(1)
        cross(1)
        ghost = plane(1, 4)
        mine = plane(0, 0)
        for n in range(16):
            face[0, n] = mine[n]
            joined = mine[n] + ghost[n]
            tot[0, n] = joined
            tot[1, 64 + n] = joined
        for b in range(1, 4):
            put(0, b, plane(0, b))

        @pl.when(coarse)
        def _():
            coarse_send(cycle)

        @pl.when(live)
        def _():
            for b in range(4):
                put(1, b, plane(1, b))

        @pl.when(jnp.logical_not(live))
        def _():
            emit(sol, sol_out, False)

        @pl.when(jnp.logical_not(coarse))
        def _():
            for b in range(4):
                update(0, b)
                update(1, b + 1)

        add_near(s)

        @pl.when(coarse)
        def _():
            add_far(s)
            correct(cycle)
            for b in range(4):
                update(0, b)
                update(1, b + 1)
            update(1, 0)

        update(0, 4)
        return 0

    lax.fori_loop(1, STEPS, step, 0)
    emit(tot, res_out, True)


def per_device(sizes, load, kappa, wet):
    layers, _, width = kappa.shape
    nodes = N * N * N
    tile = (2 * layers, width)
    half = (layers, width)
    sizes = sizes + (layers, width)
    out = jax.ShapeDtypeStruct((nodes, layers, width), F32)
    vmem = pl.BlockSpec(memory_space=pltpu.VMEM)
    fold = width // HALO
    groups = -(-N * N // fold)
    messages = 8 + 8 // fold
    dma = pltpu.SemaphoreType.DMA
    solution, residual = pl.pallas_call(
        functools.partial(kernel, sizes),
        out_shape=(out, out),
        in_specs=[vmem] * 3,
        out_specs=(vmem, vmem),
        scratch_shapes=[
            pltpu.VMEM((nodes,) + half, F32),
            pltpu.VMEM((N * groups,) + half, F32),
            pltpu.VMEM((2, N * groups) + half, F32),
            pltpu.VMEM(half, F32),
            pltpu.VMEM(half, F32),
            pltpu.VMEM((SPAN,) + tile, F32),
            pltpu.VMEM((2, 80) + tile, F32),
            pltpu.VMEM((2, 80) + tile, F32),
            pltpu.VMEM((2, 80) + tile, F32),
            pltpu.VMEM((2, 80) + tile, F32),
            pltpu.VMEM((2, nodes) + tile, F32),
            pltpu.VMEM((2, nodes) + tile, F32),
            pltpu.VMEM((2, 16) + tile, F32),
            pltpu.VMEM((STEPS, messages) + tile, F32),
            pltpu.VMEM((2, STEPS, messages) + tile, F32),
            pltpu.VMEM((CYCLES, SPAN, 2) + tile, F32),
            pltpu.VMEM((SPAN - 1,) + tile, F32),
            dma((4,)), dma((4,)), dma((SPAN + 1,)), dma((SPAN + 1,)),
            dma((2, STEPS)), dma((2, STEPS)), dma((SPAN + 1,)), dma((CYCLES, SPAN + 1)),
        ],
        compiler_params=pltpu.CompilerParams(collective_id=0, has_side_effects=True),
    )(load.reshape(nodes, layers, width), kappa.reshape(layers, width), wet.reshape(layers, width))
    return solution.reshape(load.shape), residual.reshape(load.shape)


def solution(mesh):
    sizes = tuple(mesh.shape[name] for name in ("ex", "ey", "lin"))
    field = P(None, None, None, None, ("ey", "lin"), "ex")
    cell = P(None, ("ey", "lin"), "ex")
    return jax.shard_map(
        functools.partial(per_device, sizes), mesh=mesh, in_specs=(field, cell, cell),
        out_specs=(field, field), check_vma=False,
    )
```

time: 58 us -> 51.2 us (0.88)
  Pallas kernels: 54.7 us -> 48 us
    pallas_call x1, Pallas kernels: 54.7 us -> 48 us  [per_device(): pl.pallas_call(functools.partial(kernel, sizes), out_shape=(out, out), in...]
where the time goes in v1:
time: 51.2 us; the launch traced here: 51.1 us
  Pallas kernels  48 us (94%)
  local copies, waits for them, and re-layouts  2.41 us (5%)
  between operations  0.65 us (1%)
    pallas_call x1, Pallas kernels, per_device(): pl.pallas_call(functools.partial(kernel, sizes), out_shape=(out, out), in...  48 us
    unnamed x4, local copies, waits for them, and re-layouts  2.41 us

profile of v1, /device:TPU:4, one launch (start us, length us, event | category | flops | bytes accessed | tf_op | source)
XLA Modules:
  0.0 51.1 jit_solution(16278809068949552898)
XLA Ops:
  0.6 48.0 %shard_map.50 = (f32[125,4,128]{2,1,0:T(4,128)}, f32[125,4,128]{2,1,0:T(4,128)}) custom-call(f32[125,4,128]{2,1,0:T(4,128)} %bitcast.9, f32[4,128]{1,0:T(4,128)} %bitcast.12, s32[4,128]{1,0:T(4,128)} %bitcast.13), custom_call_target="tpu_custom_call" | custom-call | tf_op jit(solution)/shard_map/pallas_call | solution.py:687
  48.6 0.0 copy-start
  48.7 1.7 %copy.9 = f32[5,5,5,4,1,128]{5,4,3,2,1,0:T(1,128)} copy(f32[5,5,5,4,1,128]{5,4,3,2,1,0:T(1,128)} %bitcast.11) | data formatting | bytes 512000
  50.4 0.0 copy-done
  50.4 0.7 %copy.10 = f32[5,5,5,4,1,128]{5,4,3,2,1,0:T(1,128)} copy(f32[5,5,5,4,1,128]{5,4,3,2,1,0:T(1,128)S(1)} %bitcast.10) | data formatting | bytes 512000
Async XLA Ops:
  48.6 1.7 %copy-start = (f32[125,4,128]{2,1,0:T(4,128)S(1)}, f32[125,4,128]{2,1,0:T(4,128)}, u32[]{:S(2)}) copy-start(f32[125,4,128]{2,1,0:T(4,128)} %get-tuple-element.5) | copy-start | bytes 768004

commit v2 on v1

--- a/solution.py
+++ b/solution.py
@@ -95,7 +95,7 @@
 def kernel(
     sizes, load_ref, kappa_ref, wet_ref, sol_out, res_out,
     ghost_load, halo_pack, halo_got, own_coeff, other_coeff, coeffs,
-    rhs, sol, tot, sinv, xs, bs, face, packed, got, cgot, cinv,
+    rhs, sol, tot, sinv, xs, bs, coarse_load, packed, got, cgot, cinv,
     ex_send, ex_recv, k_send, k_recv, f_send, f_recv, c_send, c_recv,
 ):
     ex_count, ey_count, lin_count, layers, width = sizes
@@ -312,8 +312,8 @@
             for n, x in enumerate(unpack(1, s)):
                 tot[1, n] = tot[1, n] + x
 
-    def expand(r):
-        for b in range(N):
+    def expand(r, planes):
+        for b in planes:
             w = []
             for a in range(4):
                 v = [sol[r, st(b, a, c)] for c in range(4)]
@@ -396,13 +396,13 @@
         even, odd = v[1] + v[2], float(SLOPE) * v[3]
         return even + odd, even - odd
 
-    def coarse_send(cycle):
+    def restrict_load():
         q = [[], []]
         for n in range(16):
-            v = [face[0, n], tot[0, 16 + n], tot[0, 32 + n], tot[0, 48 + n]]
+            v = [rhs[0, b * 16 + n] for b in range(N)]
             low, high = halves(v)
             q[0].append(v[0] + low)
-            q[1].append(face[1, n] + high)
+            q[1].append(v[4] + high)
         for j in range(2):
             lines = []
             for a in range(4):
@@ -410,7 +410,53 @@
                 low, high = halves(v)
                 lines.append((v[0] + low) + before(high))
             low, high = halves(lines)
-            cgot[cycle, OWN, j] = below(lines[0] + low, high)
+            coarse_load[j] = below(lines[0] + low, high)
+
+    def moments(first, mids, second):
+        even, odd = first + second, first - second
+        return (
+            float(RISE) * odd,
+            float(W0 / 2) * even + float(W1 / 2) * mids[0] + float(W2 / 4) * mids[1],
+            float(W0 / 2) * odd + float(W1 * SLOPE / (2 * KAPPA ** 2)) * mids[2],
+        )
+
+    def coarse_send(cycle):
+        along_b = []
+        for n in range(16):
+            v = [sol[0, b * 16 + n] for b in range(N)]
+            along_b.append(moments(v[0], v[1:4], v[4]))
+        mixed = [[], [], [], []]
+        plain = [[], [], [], []]
+        for c in range(4):
+            along_a = []
+            for kind in range(3):
+                v = [along_b[a * 4 + c][kind] for a in range(4)]
+                along_a.append(moments(v[0], v[1:4], above(v[0])))
+            rise, even, odd = along_a
+            mixed[1].append(rise[1])
+            mixed[2].append(even[0])
+            mixed[3].append(rise[2] + odd[0])
+            for m, x in enumerate((even[1], odd[1], even[2], odd[2])):
+                plain[m].append(x)
+        coeff = coeffs[OWN]
+        y = [None] * 4
+        for m in range(4):
+            steep = float(RISE) * (plain[m][0] - after(plain[m][0]))
+            if m == 0:
+                y[m] = (None, coeff * steep)
+            else:
+                v = mixed[m]
+                part = moments(v[0], v[1:4], after(v[0]))
+                y[m] = (coeff * part[1], coeff * (part[2] + steep))
+        for j in range(2):
+            g = []
+            for k in range(2):
+                r = []
+                for a in range(2):
+                    one, two = y[2 * a][k], y[2 * a + 1][k]
+                    r.append(plus(one, two) if j == 0 else minus(one, two))
+                g.append(below(r[0] + r[1], r[0] - r[1]))
+            cgot[cycle, OWN, j] = coarse_load[j] - ((g[0] + g[1]) + before(g[0] - g[1]))
         for d in SENDS:
             when_there(d, lambda d: remote(
                 cgot.at[cycle, OWN], cgot.at[cycle, slot_at(d)], c_send.at[REACH + d], c_recv.at[cycle, slot_at(d)],
@@ -585,6 +631,7 @@
         when_there(d, lambda d: remote(
             coeffs.at[OWN], coeffs.at[REACH + d], k_send.at[OWN], k_recv.at[REACH + d], place(d)).wait_recv())
     invert()
+    restrict_load()
     when_there(-1, lambda d: load_copy().wait())
     when_there(-1, lambda d: corner_copy().wait())
     build_rhs(1, ghost_load)
@@ -606,11 +653,15 @@
         coarse = (lax.rem(s, PERIOD) == NPRE) & live
         deferred = lax.rem(s - 1, PERIOD) != NPRE
 
-        expand(0)
+        behind = deferred & (s > 1)
+
+        @pl.when(coarse)
+        def _():
+            coarse_send(cycle)
+
+        expand(0, range(N))
         cross(0)
         mine = plane(0, 4)
-        for n in range(16):
-            face[1, n] = mine[n]
         put(0, 4, mine)
         send_face(s, mine)
 
@@ -618,28 +669,31 @@
         def _():
             far_copy(s - 1).wait_send()
 
+        @pl.when(behind)
+        def _():
+            for b in range(4):
+                put(1, b, plane(1, b))
+                if b:
+                    update(1, b)
+            update(1, 4)
+
+        for b in range(4):
+            put(0, b, plane(0, b))
+        expand(1, range(1, N))
+
         @pl.when(deferred)
         def _():
             add_far(s - 1)
             update(1, 0)
 
-        expand(1)
+        expand(1, (0,))
         cross(1)
-        ghost = plane(1, 4)
-        mine = plane(0, 0)
-        for n in range(16):
-            face[0, n] = mine[n]
-            joined = mine[n] + ghost[n]
+        for n, x in enumerate(plane(1, 4)):
+            joined = tot[0, n] + x
             tot[0, n] = joined
             tot[1, 64 + n] = joined
-        for b in range(1, 4):
-            put(0, b, plane(0, b))
 
         @pl.when(coarse)
-        def _():
-            coarse_send(cycle)
-
-        @pl.when(live)
         def _():
             for b in range(4):
                 put(1, b, plane(1, b))
@@ -652,7 +706,6 @@
         def _():
             for b in range(4):
                 update(0, b)
-                update(1, b + 1)
 
         add_near(s)
 
@@ -702,7 +755,7 @@
             pltpu.VMEM((2, 80) + tile, F32),
             pltpu.VMEM((2, nodes) + tile, F32),
             pltpu.VMEM((2, nodes) + tile, F32),
-            pltpu.VMEM((2, 16) + tile, F32),
+            pltpu.VMEM((2,) + tile, F32),
             pltpu.VMEM((STEPS, messages) + tile, F32),
             pltpu.VMEM((2, STEPS, messages) + tile, F32),
             pltpu.VMEM((CYCLES, SPAN, 2) + tile, F32),
@@ -710,7 +763,7 @@
             dma((4,)), dma((4,)), dma((SPAN + 1,)), dma((SPAN + 1,)),
             dma((2, STEPS)), dma((2, STEPS)), dma((SPAN + 1,)), dma((CYCLES, SPAN + 1)),
         ],
-        compiler_params=pltpu.CompilerParams(collective_id=0, has_side_effects=True),
+        compiler_params=pltpu.CompilerParams(collective_id=0, has_side_effects=True, vmem_limit_bytes=16 * 2 ** 20),
     )(load.reshape(nodes, layers, width), kappa.reshape(layers, width), wet.reshape(layers, width))
     return solution.reshape(load.shape), residual.reshape(load.shape)
 

time: 51.2 us -> 45.6 us (0.89)
  Pallas kernels: 48 us -> 41.8 us
  local copies, waits for them, and re-layouts: 2.41 us -> 3.03 us
    pallas_call x1, Pallas kernels: 48 us -> 41.8 us  [per_device(): pl.pallas_call(functools.partial(kernel, sizes), out_shape=(out, out), in...]
    unnamed x4 -> x8, local copies, waits for them, and re-layouts: 2.41 us -> 3.03 us
where the time goes in v2:
time: 45.6 us; the launch traced here: 45.5 us
  Pallas kernels  41.8 us (92%)
  local copies, waits for them, and re-layouts  3.03 us (7%)
  between operations  0.66 us (1%)
    pallas_call x1, Pallas kernels, per_device(): pl.pallas_call(functools.partial(kernel, sizes), out_shape=(out, out), in...  41.8 us
    unnamed x8, local copies, waits for them, and re-layouts  3.03 us

profile of v2, /device:TPU:4, one launch (start us, length us, event | category | flops | bytes accessed | tf_op | source)
XLA Modules:
  0.0 45.5 jit_solution(4044430591926828565)
XLA Ops:
  0.6 0.0 copy-start.2
  0.6 0.0 copy-start.1
  0.6 0.7 %copy-done.2 = s32[4,1,128]{2,1,0:T(1,128)S(1)} copy-done((s32[4,1,128]{2,1,0:T(1,128)S(1)}, s32[4,1,128]{2,1,0:T(1,128)}, u32[]{:S(2)}) %copy-start.2) | copy-done | bytes 2072
  1.3 0.0 copy-done.1
  1.3 0.0 copy-start
  1.3 0.9 %copy-done = f32[5,5,5,4,1,128]{5,4,3,2,1,0:T(1,128)S(1)} copy-done((f32[5,5,5,4,1,128]{5,4,3,2,1,0:T(1,128)S(1)}, f32[5,5,5,4,1,128]{5,4,3,2,1,0:T(1,128)}, u32[]{:S(2)}) %copy-start) | copy-done | bytes 256024
  2.3 41.8 %shard_map.50 = (f32[125,4,128]{2,1,0:T(4,128)S(1)}, f32[125,4,128]{2,1,0:T(4,128)S(1)}) custom-call(f32[125,4,128]{2,1,0:T(4,128)S(1)} %bitcast.9, f32[4,128]{1,0:T(4,128)S(1)} %bitcast.12, s32[4,128]{1,0:T(4,128)S(1)} %bitcast.13), custom_call_target="tpu_custom_call" | custom-call | tf_op jit(solution)/shard_map/pallas_call | solution.py:740
  44.1 0.7 %copy.9 = f32[5,5,5,4,1,128]{5,4,3,2,1,0:T(1,128)} copy(f32[5,5,5,4,1,128]{5,4,3,2,1,0:T(1,128)S(1)} %bitcast.11) | data formatting | bytes 512000
  44.8 0.7 %copy.10 = f32[5,5,5,4,1,128]{5,4,3,2,1,0:T(1,128)} copy(f32[5,5,5,4,1,128]{5,4,3,2,1,0:T(1,128)S(1)} %bitcast.10) | data formatting | bytes 512000
Async XLA Ops:
  0.6 0.7 %copy-start.2 = (s32[4,1,128]{2,1,0:T(1,128)S(1)}, s32[4,1,128]{2,1,0:T(1,128)}, u32[]{:S(2)}) copy-start(s32[4,1,128]{2,1,0:T(1,128)} %param.5) | copy-start | bytes 6148
  0.6 0.7 %copy-start.1 = (f32[4,1,128]{2,1,0:T(1,128)S(1)}, f32[4,1,128]{2,1,0:T(1,128)}, u32[]{:S(2)}) copy-start(f32[4,1,128]{2,1,0:T(1,128)} %param.4) | copy-start | bytes 6148
  1.3 0.9 %copy-start = (f32[5,5,5,4,1,128]{5,4,3,2,1,0:T(1,128)S(1)}, f32[5,5,5,4,1,128]{5,4,3,2,1,0:T(1,128)}, u32[]{:S(2)}) copy-start(f32[5,5,5,4,1,128]{5,4,3,2,1,0:T(1,128)} %param.3) | copy-start | bytes 768004

commit v3 on v2

--- a/solution.py
+++ b/solution.py
@@ -62,6 +62,8 @@
 C1, C2, C3 = CS * CE * CE, 2 * CS * CO * CE, 3 * CS * CO * CO
 SENDS = [d for d in range(-REACH + 1, REACH + 1) if d != 0]
 RECVS = [d for d in range(-REACH, REACH) if d != 0]
+NEAR_SENDS = [-1, 1, 2]
+NEAR_RECVS = [-1, 1, -2]
 
 
 def st(b, a, c):
@@ -94,9 +96,9 @@
 
 def kernel(
     sizes, load_ref, kappa_ref, wet_ref, sol_out, res_out,
-    ghost_load, halo_pack, halo_got, own_coeff, other_coeff, coeffs,
+    load, part, got_part, got_halo, halves_of, coeffs,
     rhs, sol, tot, sinv, xs, bs, coarse_load, packed, got, cgot, cinv,
-    ex_send, ex_recv, k_send, k_recv, f_send, f_recv, c_send, c_recv,
+    load_sem, x_send, x_recv, k_send, k_recv, f_send, f_recv, c_send, c_recv,
 ):
     ex_count, ey_count, lin_count, layers, width = sizes
     ex, ey, lin = lax.axis_index("ex"), lax.axis_index("ey"), lax.axis_index("lin")
@@ -105,7 +107,7 @@
     par = lax.rem(lin, 2)
     sgn = 1 - 2 * par
     fold = width // HALO
-    groups = -(-N * N // fold)
+    groups = 80 // fold
 
     sub = lax.broadcasted_iota(jnp.int32, (2 * layers, width), 0)
     lane = lax.broadcasted_iota(jnp.int32, (2 * layers, width), 1)
@@ -150,83 +152,41 @@
         return pltpu.make_async_remote_copy(
             src_ref=src, dst_ref=dst, send_sem=send, recv_sem=recv, device_id=device, device_id_type=MESH)
 
-    coeffs[...] = jnp.zeros_like(coeffs)
+    fetch = pltpu.make_async_copy(load_ref, load, load_sem)
+    fetch.start()
+    halves_of[...] = jnp.zeros_like(halves_of)
     cgot[...] = jnp.zeros_like(cgot)
 
     @pl.when(jnp.logical_not(there(-1)))
     def _():
-        ghost_load[...] = jnp.zeros_like(ghost_load)
-        halo_got[1] = jnp.zeros_like(halo_got[1])
+        got_part[...] = jnp.zeros_like(got_part)
+        got_halo[1] = jnp.zeros_like(got_halo[1])
 
     def greet(device):
         pl.semaphore_signal(pltpu.get_barrier_semaphore(), inc=1, device_id=device, device_id_type=MESH)
 
     greet((1 - ex, ey, lin))
-    when_there(-1, lambda d: greet(place(d, True)))
-    expected = 1 + there(-1).astype(jnp.int32)
+    expected = jnp.int32(1)
     for d in range(1, REACH + 1):
         for e in (-d, d):
-            when_there(e, lambda e: greet(place(e)))
-            expected = expected + there(e).astype(jnp.int32)
-
-    coeff_own = kappa_ref[...] * jnp.where(wet_ref[...] == 1, F32(1.0), F32(0.05))
-    own_coeff[...] = coeff_own
+            @pl.when(there(e))
+            def _():
+                greet(place(e))
+                if d <= 2:
+                    greet(place(e, True))
+            expected = expected + jnp.where(there(e), 2 if d <= 2 else 1, 0)
+
+    halves_of[0, OWN] = kappa_ref[...] * jnp.where(wet_ref[...] == 1, F32(1.0), F32(0.05))
 
     def raw(a, b, c):
         return (a * N + b + par * (N - 1 - 2 * b)) * N + c
 
-    half_lane = lax.broadcasted_iota(jnp.int32, (layers, width), 1)
-    source = jnp.where(ex == 0, fold - 1, 0)
-    turn = (half_lane // HALO + fold - source) % fold
-
-    def pack_plane(b, _):
-        for g in range(groups):
-            mixed = None
-            for j in range(fold):
-                n = g * fold + j
-                if n < N * N:
-                    x = load_ref[raw(n // N, b, n % N)]
-                    mixed = x if j == 0 else jnp.where(turn == j, pltpu.roll(x, HALO * j, 1), mixed)
-            halo_pack[b * groups + g] = mixed
-        return 0
-
-    lax.fori_loop(0, N, pack_plane, 0)
-    pl.semaphore_wait(pltpu.get_barrier_semaphore(), expected)
-
-    across = (1 - ex, ey, lin)
-    coeff_copy = remote(own_coeff, other_coeff, ex_send.at[0], ex_recv.at[0], across)
-    halo_copy = remote(halo_pack, halo_got.at[0], ex_send.at[1], ex_recv.at[1], across)
-
-    def load_copy():
-        return remote(load_ref, ghost_load, ex_send.at[2], ex_recv.at[2], place(-1))
-
-    def corner_copy():
-        return remote(halo_pack, halo_got.at[1], ex_send.at[3], ex_recv.at[3], place(-1, True))
-
-    coeff_copy.start()
-    halo_copy.start()
-    when_there(-1, lambda d: load_copy().start())
-    when_there(-1, lambda d: corner_copy().start())
-
-    coeff_copy.wait()
-    coeffs[OWN] = jnp.where(real, jnp.concatenate([coeff_own, other_coeff[...]], axis=0), 0.0)
-    for d in SENDS:
-        when_there(d, lambda d: remote(
-            coeffs.at[OWN], coeffs.at[slot_at(d)], k_send.at[REACH + d], k_recv.at[slot_at(d)], place(d)).start())
-
     def to_dual(f):
         return [(f[1] + f[3]) * 0.5, f[2] * 0.5, (f[1] - f[3]) * float(0.5 / KAPPA)]
 
-    def load_plane(r, b, own_ref):
-        source_b = b if r == 0 else N - 1 - b
-        tiles = []
-        for n in range(N * N):
-            mine = own_ref[raw(n // N, b, n % N)]
-            other = halo_got[r, source_b * groups + n // fold]
-            j = n % fold
-            if j:
-                other = pltpu.roll(other, width - HALO * j, 1)
-            tiles.append(jnp.where(real, jnp.concatenate([mine, other], axis=0), 0.0))
+    def load_plane(b):
+        nothing = jnp.zeros((layers, width), F32)
+        tiles = [jnp.concatenate([load[raw(n // N, b, n % N)], nothing], axis=0) for n in range(N * N)]
         lines = []
         for a in range(N):
             f = tiles[a * N:a * N + N]
@@ -235,25 +195,95 @@
         for c in range(4):
             f = [lines[a][c] for a in range(N)]
             columns.append([below(f[0], f[4])] + to_dual(f))
-        return [[columns[c][a] for c in range(4)] for a in range(4)]
-
-    def build_rhs(r, own_ref):
-        for b, at in ((0, 0), (4, 4), (2, 2), (1, 1), (3, 3)):
-            p = load_plane(r, b, own_ref)
-            for a in range(4):
-                for c in range(4):
-                    x = p[a][c]
-                    if b == 2:
-                        x = x * 0.5
-                    if b == 3:
-                        first = rhs[r, st(1, a, c)]
-                        rhs[r, st(3, a, c)] = (first - x) * float(0.5 / KAPPA)
-                        rhs[r, st(1, a, c)] = (first + x) * 0.5
-                    else:
-                        rhs[r, st(at, a, c)] = x
-
-    halo_copy.wait()
-    build_rhs(0, load_ref)
+        return [columns[c][a] for a in range(4) for c in range(4)]
+
+    fetch.wait()
+    for b in (0, 4, 2, 1, 3):
+        for n, x in enumerate(load_plane(b)):
+            if b == 3:
+                first = rhs[0, 16 + n]
+                rhs[0, 48 + n] = (first - x) * float(0.5 / KAPPA)
+                rhs[0, 16 + n] = (first + x) * 0.5
+            else:
+                rhs[0, b * 16 + n] = x * 0.5 if b == 2 else x
+    source = jnp.where(ex == 0, fold - 1, 0)
+    turn = (lane // HALO + fold - source) % fold
+    for g in range(groups):
+        mixed = None
+        for j in range(fold):
+            x = rhs[0, g * fold + j]
+            part[groups + 1 + g * fold + j] = x[0:layers]
+            mixed = x if j == 0 else jnp.where(turn == j, pltpu.roll(x, HALO * j, 1), mixed)
+        part[g] = mixed[0:layers]
+    mixed = None
+    for j in range(20):
+        x = rhs[0, 4 * j]
+        mixed = x if j == 0 else jnp.where(lane == j, pltpu.roll(x, j, 1), mixed)
+    part[groups] = pltpu.roll(mixed, layers, 0)[0:layers]
+
+    pl.semaphore_wait(pltpu.get_barrier_semaphore(), expected)
+
+    def half_copy(h, d, slot, device, source=0):
+        return remote(halves_of.at[source, OWN], halves_of.at[h, slot], k_send.at[h, REACH + d], k_recv.at[h, slot],
+                      device)
+
+    def half_sent(h, d):
+        half_copy(h, d, OWN, place(d), h).wait_send()
+
+    def half_came(h, d):
+        half_copy(h, d, REACH + d, place(d), h).wait_recv()
+
+    half_copy(1, 0, OWN, place(0, True)).start()
+    for d in NEAR_SENDS:
+        @pl.when(there(d))
+        def _():
+            half_copy(0, d, slot_at(d), place(d)).start()
+            half_copy(1, d, slot_at(d), place(d, True)).start()
+
+    def halo_copy(kind, device):
+        return remote(part.at[0:groups + 1], got_halo.at[kind], x_send.at[kind], x_recv.at[kind], device)
+
+    def part_copy(k):
+        at, size = ((0, 17), (17, 64))[k]
+        return remote(part.at[groups + at:groups + at + size], got_part.at[at:at + size], x_send.at[2 + k],
+                      x_recv.at[2 + k], place(-1))
+
+    halo_copy(0, place(0, True)).start()
+
+    @pl.when(there(-1))
+    def _():
+        part_copy(0).start()
+        halo_copy(1, place(-1, True)).start()
+        part_copy(1).start()
+
+    for d in SENDS:
+        if d not in NEAR_SENDS:
+            when_there(d, lambda d: half_copy(0, d, slot_at(d), place(d)).start())
+
+    outer = (sub >= layers) & (near < HALO)
+    entering = first_lane & ((sub >= layers) | (ex == 1))
+
+    def assemble(r, b):
+        source_b = b if r == 0 or 0 < b < 4 else 4 - b
+        nothing = jnp.zeros((layers, width), F32)
+        spill = jnp.concatenate([got_halo[r, groups], got_part[0] if r else nothing], axis=0)
+        for a in range(4):
+            for c in range(4):
+                n, m = st(b, a, c), st(source_b, a, c)
+                h = got_halo[r, m // fold]
+                h = jnp.concatenate([h, h], axis=0)
+                if m % fold:
+                    h = pltpu.roll(h, width - HALO * (m % fold), 1)
+                h = jnp.where(outer, h, 0.0)
+                if r == 0:
+                    x = rhs[0, n] + h
+                else:
+                    p = got_part[1 + m]
+                    x = jnp.where(lower, jnp.concatenate([p, p], axis=0), h)
+                if c == 0:
+                    j = m // 4
+                    x = x + jnp.where(entering, pltpu.roll(spill, width - j, 1) if j else spill, 0.0)
+                rhs[r, n] = -x if r == 1 and b == 3 else x
 
     block = lax.rem(lane + jnp.where(ex == 0, 0, HALO - 1), width) // HALO
 
@@ -386,6 +416,25 @@
                         for c in range(4):
                             factor = FINE_RELAX * NU[a] * NU[b] * NU[c] / K3[NODE[a], NODE[b], NODE[c]]
                             sinv[r, st(b, a, c)] = float(factor) * tiles[min(a, 1)][min(c, 1)]
+
+    def join_coeff(e):
+        coeffs[e] = jnp.where(real, jnp.concatenate([halves_of[0, e], halves_of[1, e]], axis=0), 0.0)
+
+    def coarse_invert():
+        for d in SENDS:
+            @pl.when(there(d))
+            def _():
+                half_sent(0, d)
+                half_sent(1, d)
+        for d in RECVS:
+            if d not in NEAR_RECVS:
+                @pl.when(there(d))
+                def _():
+                    half_came(0, d)
+                    half_came(1, d)
+        for e in range(SPAN):
+            if abs(e - OWN + 0.5) > 2:
+                join_coeff(e)
         corner = 3.0 * SC[0, 0] * WC[0, 0] ** 2
         for i in range(SPAN - 1):
             pair = coeffs[i] + coeffs[i + 1]
@@ -463,6 +512,10 @@
                 place(d)).start())
 
     def correct(cycle):
+        @pl.when(cycle == 0)
+        def _():
+            coarse_invert()
+
         for d in SENDS:
             when_there(d, lambda d: remote(
                 cgot.at[cycle, OWN], cgot.at[cycle, OWN], c_send.at[REACH + d], c_recv.at[cycle, OWN],
@@ -620,30 +673,39 @@
         for b in range(1, 4):
             one(b, [v[b - 1] for v in mids])
 
-    for b in range(N):
+    halo_copy(0, place(0, True)).wait()
+    for b in (4, 0, 1, 2, 3):
+        assemble(0, b)
         put(0, b, [rhs[0, b * 16 + n] for n in range(16)])
-    send_face(0, [tot[0, 64 + n] for n in range(16)])
+        if b == 4:
+            send_face(0, [tot[0, 64 + n] for n in range(16)])
     sol[...] = jnp.zeros_like(sol)
+    half_copy(1, 0, OWN, place(0, True)).wait()
     for d in SENDS:
-        when_there(d, lambda d: remote(
-            coeffs.at[OWN], coeffs.at[OWN], k_send.at[REACH + d], k_recv.at[OWN], place(d)).wait_send())
-    for d in RECVS:
-        when_there(d, lambda d: remote(
-            coeffs.at[OWN], coeffs.at[REACH + d], k_send.at[OWN], k_recv.at[REACH + d], place(d)).wait_recv())
+        if d not in NEAR_SENDS:
+            when_there(d, lambda d: half_copy(1, d, slot_at(d), place(d), 1).start())
+    for d in NEAR_RECVS:
+        @pl.when(there(d))
+        def _():
+            half_came(0, d)
+            half_came(1, d)
+    for e in range(OWN - 2, OWN + 2):
+        join_coeff(e)
     invert()
     restrict_load()
-    when_there(-1, lambda d: load_copy().wait())
-    when_there(-1, lambda d: corner_copy().wait())
-    build_rhs(1, ghost_load)
-    for b in range(N):
-        put(1, b, [rhs[1, b * 16 + n] for n in range(16)])
+
+    @pl.when(there(-1))
+    def _():
+        part_copy(0).wait()
+        halo_copy(1, place(-1, True)).wait()
+
+    assemble(1, 4)
     for n in range(16):
-        joined = tot[0, n] + tot[1, 64 + n]
+        joined = tot[0, n] + rhs[1, 64 + n]
         tot[0, n] = joined
         tot[1, 64 + n] = joined
     for b in range(4):
         update(0, b)
-        update(1, b + 1)
     add_near(0)
     update(0, 4)
 
@@ -679,6 +741,17 @@
 
         for b in range(4):
             put(0, b, plane(0, b))
+
+        @pl.when(s == 1)
+        def _():
+            when_there(-1, lambda d: part_copy(1).wait())
+            for b in range(4):
+                assemble(1, b)
+                put(1, b, [rhs[1, b * 16 + n] for n in range(16)])
+                if b:
+                    update(1, b)
+            update(1, 4)
+
         expand(1, range(1, N))
 
         @pl.when(deferred)
@@ -734,20 +807,20 @@
     out = jax.ShapeDtypeStruct((nodes, layers, width), F32)
     vmem = pl.BlockSpec(memory_space=pltpu.VMEM)
     fold = width // HALO
-    groups = -(-N * N // fold)
+    groups = 80 // fold
     messages = 8 + 8 // fold
     dma = pltpu.SemaphoreType.DMA
     solution, residual = pl.pallas_call(
         functools.partial(kernel, sizes),
         out_shape=(out, out),
-        in_specs=[vmem] * 3,
+        in_specs=[pl.BlockSpec(memory_space=pltpu.HBM), vmem, vmem],
         out_specs=(vmem, vmem),
         scratch_shapes=[
             pltpu.VMEM((nodes,) + half, F32),
-            pltpu.VMEM((N * groups,) + half, F32),
-            pltpu.VMEM((2, N * groups) + half, F32),
-            pltpu.VMEM(half, F32),
-            pltpu.VMEM(half, F32),
+            pltpu.VMEM((groups + 81,) + half, F32),
+            pltpu.VMEM((81,) + half, F32),
+            pltpu.VMEM((2, groups + 1) + half, F32),
+            pltpu.VMEM((2, SPAN + 1) + half, F32),
             pltpu.VMEM((SPAN,) + tile, F32),
             pltpu.VMEM((2, 80) + tile, F32),
             pltpu.VMEM((2, 80) + tile, F32),
@@ -760,7 +833,7 @@
             pltpu.VMEM((2, STEPS, messages) + tile, F32),
             pltpu.VMEM((CYCLES, SPAN, 2) + tile, F32),
             pltpu.VMEM((SPAN - 1,) + tile, F32),
-            dma((4,)), dma((4,)), dma((SPAN + 1,)), dma((SPAN + 1,)),
+            dma, dma((4,)), dma((4,)), dma((2, SPAN + 1)), dma((2, SPAN + 1)),
             dma((2, STEPS)), dma((2, STEPS)), dma((SPAN + 1,)), dma((CYCLES, SPAN + 1)),
         ],
         compiler_params=pltpu.CompilerParams(collective_id=0, has_side_effects=True, vmem_limit_bytes=16 * 2 ** 20),

time: 45.6 us -> 41.1 us (0.901)
  Pallas kernels: 41.8 us -> 37.2 us
    pallas_call x1, Pallas kernels: 41.8 us -> 37.2 us  [per_device(): pl.pallas_call(functools.partial(kernel, sizes), out_shape=(out, out), in...]
where the time goes in v3:
time: 41.1 us; the launch traced here: 40.9 us
  Pallas kernels  37.2 us (91%)
  local copies, waits for them, and re-layouts  3.03 us (7%)
  between operations  0.66 us (2%)
    pallas_call x1, Pallas kernels, per_device(): pl.pallas_call(functools.partial(kernel, sizes), out_shape=(out, out), in...  37.2 us
    unnamed x8, local copies, waits for them, and re-layouts  3.03 us

profile of v3, /device:TPU:4, one launch (start us, length us, event | category | flops | bytes accessed | tf_op | source)
XLA Modules:
  0.0 40.9 jit_solution(14461563990839715672)
XLA Ops:
  0.6 0.0 copy-start.2
  0.6 0.0 copy-start.1
  0.6 0.7 %copy-done.2 = s32[4,1,128]{2,1,0:T(1,128)S(1)} copy-done((s32[4,1,128]{2,1,0:T(1,128)S(1)}, s32[4,1,128]{2,1,0:T(1,128)}, u32[]{:S(2)}) %copy-start.2) | copy-done | bytes 2072
  1.3 0.0 copy-done.1
  1.3 0.0 copy-start
  1.3 0.9 %copy-done = f32[5,5,5,4,1,128]{5,4,3,2,1,0:T(1,128)S(1)} copy-done((f32[5,5,5,4,1,128]{5,4,3,2,1,0:T(1,128)S(1)}, f32[5,5,5,4,1,128]{5,4,3,2,1,0:T(1,128)}, u32[]{:S(2)}) %copy-start) | copy-done | bytes 256024
  2.3 37.2 %shard_map.50 = (f32[125,4,128]{2,1,0:T(4,128)S(1)}, f32[125,4,128]{2,1,0:T(4,128)S(1)}) custom-call(f32[125,4,128]{2,1,0:T(4,128)S(1)} %bitcast.9, f32[4,128]{1,0:T(4,128)S(1)} %bitcast.12, s32[4,128]{1,0:T(4,128)S(1)} %bitcast.13), custom_call_target="tpu_custom_call" | custom-call | tf_op jit(solution)/shard_map/pallas_call | solution.py:813
  39.5 0.7 %copy.9 = f32[5,5,5,4,1,128]{5,4,3,2,1,0:T(1,128)} copy(f32[5,5,5,4,1,128]{5,4,3,2,1,0:T(1,128)S(1)} %bitcast.11) | data formatting | bytes 512000
  40.2 0.7 %copy.10 = f32[5,5,5,4,1,128]{5,4,3,2,1,0:T(1,128)} copy(f32[5,5,5,4,1,128]{5,4,3,2,1,0:T(1,128)S(1)} %bitcast.10) | data formatting | bytes 512000
Async XLA Ops:
  0.6 0.7 %copy-start.2 = (s32[4,1,128]{2,1,0:T(1,128)S(1)}, s32[4,1,128]{2,1,0:T(1,128)}, u32[]{:S(2)}) copy-start(s32[4,1,128]{2,1,0:T(1,128)} %param.5) | copy-start | bytes 6148
  0.6 0.7 %copy-start.1 = (f32[4,1,128]{2,1,0:T(1,128)S(1)}, f32[4,1,128]{2,1,0:T(1,128)}, u32[]{:S(2)}) copy-start(f32[4,1,128]{2,1,0:T(1,128)} %param.4) | copy-start | bytes 6148
  1.3 0.9 %copy-start = (f32[5,5,5,4,1,128]{5,4,3,2,1,0:T(1,128)S(1)}, f32[5,5,5,4,1,128]{5,4,3,2,1,0:T(1,128)}, u32[]{:S(2)}) copy-start(f32[5,5,5,4,1,128]{5,4,3,2,1,0:T(1,128)} %param.3) | copy-start | bytes 768004

commit v4 on v3

--- a/solution.py
+++ b/solution.py
@@ -96,7 +96,7 @@
 
 def kernel(
     sizes, load_ref, kappa_ref, wet_ref, sol_out, res_out,
-    load, part, got_part, got_halo, halves_of, coeffs,
+    load, kappa, wet, part, got_part, got_halo, halves_of, coeffs,
     rhs, sol, tot, sinv, xs, bs, coarse_load, packed, got, cgot, cinv,
     load_sem, x_send, x_recv, k_send, k_recv, f_send, f_recv, c_send, c_recv,
 ):
@@ -108,6 +108,7 @@
     sgn = 1 - 2 * par
     fold = width // HALO
     groups = 80 // fold
+    first = 16 // fold
 
     sub = lax.broadcasted_iota(jnp.int32, (2 * layers, width), 0)
     lane = lax.broadcasted_iota(jnp.int32, (2 * layers, width), 1)
@@ -152,8 +153,10 @@
         return pltpu.make_async_remote_copy(
             src_ref=src, dst_ref=dst, send_sem=send, recv_sem=recv, device_id=device, device_id_type=MESH)
 
-    fetch = pltpu.make_async_copy(load_ref, load, load_sem)
-    fetch.start()
+    fetches = [pltpu.make_async_copy(src, dst, load_sem.at[k]) for k, (src, dst) in enumerate(
+        ((kappa_ref, kappa), (wet_ref, wet), (load_ref, load)))]
+    for fetch in fetches:
+        fetch.start()
     halves_of[...] = jnp.zeros_like(halves_of)
     cgot[...] = jnp.zeros_like(cgot)
 
@@ -176,7 +179,9 @@
                     greet(place(e, True))
             expected = expected + jnp.where(there(e), 2 if d <= 2 else 1, 0)
 
-    halves_of[0, OWN] = kappa_ref[...] * jnp.where(wet_ref[...] == 1, F32(1.0), F32(0.05))
+    fetches[0].wait()
+    fetches[1].wait()
+    halves_of[0, OWN] = kappa[...] * jnp.where(wet[...] == 1, F32(1.0), F32(0.05))
 
     def raw(a, b, c):
         return (a * N + b + par * (N - 1 - 2 * b)) * N + c
@@ -197,29 +202,33 @@
             columns.append([below(f[0], f[4])] + to_dual(f))
         return [columns[c][a] for a in range(4) for c in range(4)]
 
-    fetch.wait()
+    fetches[2].wait()
     for b in (0, 4, 2, 1, 3):
         for n, x in enumerate(load_plane(b)):
             if b == 3:
-                first = rhs[0, 16 + n]
-                rhs[0, 48 + n] = (first - x) * float(0.5 / KAPPA)
-                rhs[0, 16 + n] = (first + x) * 0.5
+                other = rhs[0, 16 + n]
+                rhs[0, 48 + n] = (other - x) * float(0.5 / KAPPA)
+                rhs[0, 16 + n] = (other + x) * 0.5
             else:
                 rhs[0, b * 16 + n] = x * 0.5 if b == 2 else x
+    def at_group(g):
+        return g if g < first else g + 1
+
     source = jnp.where(ex == 0, fold - 1, 0)
     turn = (lane // HALO + fold - source) % fold
     for g in range(groups):
         mixed = None
         for j in range(fold):
             x = rhs[0, g * fold + j]
-            part[groups + 1 + g * fold + j] = x[0:layers]
+            part[groups + 2 + g * fold + j] = x[0:layers]
             mixed = x if j == 0 else jnp.where(turn == j, pltpu.roll(x, HALO * j, 1), mixed)
-        part[g] = mixed[0:layers]
+        part[at_group(g)] = mixed[0:layers]
     mixed = None
     for j in range(20):
         x = rhs[0, 4 * j]
         mixed = x if j == 0 else jnp.where(lane == j, pltpu.roll(x, j, 1), mixed)
-    part[groups] = pltpu.roll(mixed, layers, 0)[0:layers]
+    for at in (first, groups + 1):
+        part[at] = pltpu.roll(mixed, layers, 0)[0:layers]
 
     pl.semaphore_wait(pltpu.get_barrier_semaphore(), expected)
 
@@ -240,21 +249,24 @@
             half_copy(0, d, slot_at(d), place(d)).start()
             half_copy(1, d, slot_at(d), place(d, True)).start()
 
-    def halo_copy(kind, device):
-        return remote(part.at[0:groups + 1], got_halo.at[kind], x_send.at[kind], x_recv.at[kind], device)
+    def halo_copy(k):
+        at, size = ((0, groups + 1), (0, first + 1), (first + 1, groups - first))[k]
+        return remote(part.at[at:at + size], got_halo.at[min(k, 1), at:at + size], x_send.at[k], x_recv.at[k],
+                      place(-1 if k else 0, True))
 
     def part_copy(k):
         at, size = ((0, 17), (17, 64))[k]
-        return remote(part.at[groups + at:groups + at + size], got_part.at[at:at + size], x_send.at[2 + k],
-                      x_recv.at[2 + k], place(-1))
-
-    halo_copy(0, place(0, True)).start()
+        return remote(part.at[groups + 1 + at:groups + 1 + at + size], got_part.at[at:at + size], x_send.at[3 + k],
+                      x_recv.at[3 + k], place(-1))
+
+    halo_copy(0).start()
 
     @pl.when(there(-1))
     def _():
+        halo_copy(1).start()
         part_copy(0).start()
-        halo_copy(1, place(-1, True)).start()
         part_copy(1).start()
+        halo_copy(2).start()
 
     for d in SENDS:
         if d not in NEAR_SENDS:
@@ -266,11 +278,11 @@
     def assemble(r, b):
         source_b = b if r == 0 or 0 < b < 4 else 4 - b
         nothing = jnp.zeros((layers, width), F32)
-        spill = jnp.concatenate([got_halo[r, groups], got_part[0] if r else nothing], axis=0)
+        spill = jnp.concatenate([got_halo[r, first], got_part[0] if r else nothing], axis=0)
         for a in range(4):
             for c in range(4):
                 n, m = st(b, a, c), st(source_b, a, c)
-                h = got_halo[r, m // fold]
+                h = got_halo[r, at_group(m // fold)]
                 h = jnp.concatenate([h, h], axis=0)
                 if m % fold:
                     h = pltpu.roll(h, width - HALO * (m % fold), 1)
@@ -540,11 +552,11 @@
                 parts.append((k + high, k - high))
             return [[parts[k][i] for k in range(2)] for i in range(2)]
 
-        first, last = 0, lines - 1
+        begin, end = 0, lines - 1
         for sweep in range(NC - 1):
-            m = {i: modes(x[i]) for i in range(first, last + 1)}
+            m = {i: modes(x[i]) for i in range(begin, end + 1)}
             sides = {}
-            for e in range(first + 1, last + 1):
+            for e in range(begin + 1, end + 1):
                 coeff = coeffs[e]
                 factor = [float(C1) * coeff, float(C2) * coeff, float(C3) * coeff]
                 low, high = m[e - 1], m[e]
@@ -560,9 +572,9 @@
                             pair.append((even + odd, even - odd))
                     part.append(pair)
                 sides[e] = part
-            first, last = first + 1, last - 1
+            begin, end = begin + 1, end - 1
             new = list(x)
-            for i in range(first, last + 1):
+            for i in range(begin, end + 1):
                 y = [[sides[i + 1][a][k][0] + sides[i][a][k][1] for k in range(2)] for a in range(2)]
                 g = [below(y[0][k] + y[1][k], y[0][k] - y[1][k]) for k in range(2)]
                 image = (g[0] + g[1]) + before(g[0] - g[1])
@@ -673,7 +685,7 @@
         for b in range(1, 4):
             one(b, [v[b - 1] for v in mids])
 
-    halo_copy(0, place(0, True)).wait()
+    halo_copy(0).wait()
     for b in (4, 0, 1, 2, 3):
         assemble(0, b)
         put(0, b, [rhs[0, b * 16 + n] for n in range(16)])
@@ -697,7 +709,7 @@
     @pl.when(there(-1))
     def _():
         part_copy(0).wait()
-        halo_copy(1, place(-1, True)).wait()
+        halo_copy(1).wait()
 
     assemble(1, 4)
     for n in range(16):
@@ -744,7 +756,11 @@
 
         @pl.when(s == 1)
         def _():
-            when_there(-1, lambda d: part_copy(1).wait())
+            @pl.when(there(-1))
+            def _():
+                part_copy(1).wait()
+                halo_copy(2).wait()
+
             for b in range(4):
                 assemble(1, b)
                 put(1, b, [rhs[1, b * 16 + n] for n in range(16)])
@@ -813,11 +829,13 @@
     solution, residual = pl.pallas_call(
         functools.partial(kernel, sizes),
         out_shape=(out, out),
-        in_specs=[pl.BlockSpec(memory_space=pltpu.HBM), vmem, vmem],
+        in_specs=[pl.BlockSpec(memory_space=pltpu.HBM)] * 3,
         out_specs=(vmem, vmem),
         scratch_shapes=[
             pltpu.VMEM((nodes,) + half, F32),
-            pltpu.VMEM((groups + 81,) + half, F32),
+            pltpu.VMEM(half, F32),
+            pltpu.VMEM(half, jnp.int32),
+            pltpu.VMEM((groups + 82,) + half, F32),
             pltpu.VMEM((81,) + half, F32),
             pltpu.VMEM((2, groups + 1) + half, F32),
             pltpu.VMEM((2, SPAN + 1) + half, F32),
@@ -833,11 +851,12 @@
             pltpu.VMEM((2, STEPS, messages) + tile, F32),
             pltpu.VMEM((CYCLES, SPAN, 2) + tile, F32),
             pltpu.VMEM((SPAN - 1,) + tile, F32),
-            dma, dma((4,)), dma((4,)), dma((2, SPAN + 1)), dma((2, SPAN + 1)),
+            dma((3,)), dma((5,)), dma((5,)), dma((2, SPAN + 1)), dma((2, SPAN + 1)),
             dma((2, STEPS)), dma((2, STEPS)), dma((SPAN + 1,)), dma((CYCLES, SPAN + 1)),
         ],
         compiler_params=pltpu.CompilerParams(collective_id=0, has_side_effects=True, vmem_limit_bytes=16 * 2 ** 20),
-    )(load.reshape(nodes, layers, width), kappa.reshape(layers, width), wet.reshape(layers, width))
+    )(*[pltpu.with_memory_space_constraint(x, pltpu.HBM) for x in (
+        load.reshape(nodes, layers, width), kappa.reshape(layers, width), wet.reshape(layers, width))])
     return solution.reshape(load.shape), residual.reshape(load.shape)
 
 

time: 41.1 us -> 39.1 us (0.951)
  local copies, waits for them, and re-layouts: 3.03 us -> 1.4 us
    unnamed x8 -> x2, local copies, waits for them, and re-layouts: 3.03 us -> 1.4 us
where the time goes in v4:
time: 39.1 us; the launch traced here: 38.9 us
  Pallas kernels  36.9 us (94%)
  local copies, waits for them, and re-layouts  1.4 us (4%)
  between operations  0.64 us (2%)
    pallas_call x1, Pallas kernels, per_device(): pl.pallas_call(functools.partial(kernel, sizes), out_shape=(out, out), in...  36.9 us
    unnamed x2, local copies, waits for them, and re-layouts  1.4 us

profile of v4, /device:TPU:4, one launch (start us, length us, event | category | flops | bytes accessed | tf_op | source)
XLA Modules:
  0.0 38.9 jit_solution(3458069388672180267)
XLA Ops:
  0.6 36.9 %shard_map.50 = (f32[125,4,128]{2,1,0:T(4,128)S(1)}, f32[125,4,128]{2,1,0:T(4,128)S(1)}) custom-call(f32[125,4,128]{2,1,0:T(4,128)} %bitcast.11, f32[4,128]{1,0:T(4,128)} %bitcast.12, s32[4,128]{1,0:T(4,128)} %bitcast.13), custom_call_target="tpu_custom_call" | custom-call | tf_op jit(solution)/shard_map/pallas_call | solution.py:829
  37.5 0.7 %copy.9 = f32[5,5,5,4,1,128]{5,4,3,2,1,0:T(1,128)} copy(f32[5,5,5,4,1,128]{5,4,3,2,1,0:T(1,128)S(1)} %bitcast.10) | data formatting | bytes 512000
  38.2 0.7 %copy.10 = f32[5,5,5,4,1,128]{5,4,3,2,1,0:T(1,128)} copy(f32[5,5,5,4,1,128]{5,4,3,2,1,0:T(1,128)S(1)} %bitcast.9) | data formatting | bytes 512000

commit v5 on v4

--- a/solution.py
+++ b/solution.py
@@ -97,7 +97,7 @@
 def kernel(
     sizes, load_ref, kappa_ref, wet_ref, sol_out, res_out,
     load, kappa, wet, part, got_part, got_halo, halves_of, coeffs,
-    rhs, sol, tot, sinv, xs, bs, coarse_load, packed, got, cgot, cinv,
+    rhs, sol, tot, sinv, xs, bs, coarse_load, shares, packed, got, cgot, cinv,
     load_sem, x_send, x_recv, k_send, k_recv, f_send, f_recv, c_send, c_recv,
 ):
     ex_count, ey_count, lin_count, layers, width = sizes
@@ -373,7 +373,7 @@
             for k in range(N):
                 v = [xs[r, xi(b, i, k)] for b in range(N)]
                 r0, r1, rz, s1, s0 = line_apply(v[0] + v[4], v[1], v[2], v[3], v[0] - v[4], MU[i] * MU[k])
-                for b, x in enumerate((r0 + s0, r1, rz, s1, r0 - s0)):
+                for b, x in enumerate((r0 + s0, r1, rz, s1)):
                     bs[r, xi(b, i, k)] = x
 
     def gather(y):
@@ -387,6 +387,12 @@
             h.append([None if low is None else low + before(high)] + [g[k][a] for k in range(1, 4)])
         return h
 
+    def top_term(r, i, k):
+        v = [xs[r, xi(b, i, k)] for b in range(N)]
+        scale = MU[i] * MU[k]
+        r0 = float(ALPHA * scale) * (v[0] + v[4] - v[2]) + float(BETA * scale) * (v[1] - v[2])
+        return r0 - float(ODD * scale) * ((v[0] - v[4]) + v[3])
+
     def plane(r, b):
         coeff = coeffs[OWN - r]
         x = [[xs[r, xi(b, i, k)] for k in range(N)] for i in range(N)]
@@ -396,7 +402,8 @@
         for i in range(N):
             line = []
             for k in range(N):
-                terms = sorted(((b == 2, bs[r, xi(b, i, k)]), (k == 2, along_c[i][k]), (i == 2, along_a[k][i])),
+                along_b = top_term(r, i, k) if b == 4 else bs[r, xi(b, i, k)]
+                terms = sorted(((b == 2, along_b), (k == 2, along_c[i][k]), (i == 2, along_a[k][i])),
                                key=lambda t: t[0])
                 total = -terms[0][1] if terms[0][0] else terms[0][1]
                 for negative, term in terms[1:]:
@@ -420,6 +427,9 @@
     def invert():
         for r in range(2):
             here = coeffs[OWN - r]
+            two = here + before(here)
+            for k, x in enumerate((here, two, below(here, here), below(two, two))):
+                shares[r, k] = x
             for bl, x in (((1, 2, 3), here), ((0,), here + coeffs[OWN - r - 1]), ((4,), here + coeffs[OWN - r + 1])):
                 xc = x + before(x)
                 tiles = [[inverted(below(xc, xc)), inverted(below(x, x))], [inverted(xc), inverted(x)]]
@@ -428,6 +438,13 @@
                         for c in range(4):
                             factor = FINE_RELAX * NU[a] * NU[b] * NU[c] / K3[NODE[a], NODE[b], NODE[c]]
                             sinv[r, st(b, a, c)] = float(factor) * tiles[min(a, 1)][min(c, 1)]
+
+    def shift_top(r, at, n):
+        delta = sinv[r, n] * tot[r, n]
+        sol[r, n] = sol[r, n] + delta
+        a, c = n // 4, n % 4
+        factor = S[4, 0] * (MU[a] if a else W0) * (MU[c] if c else W0)
+        tot[r, at + n] = tot[r, at + n] - float(factor) * shares[r, (0 if a else 2) + (0 if c else 1)] * delta
 
     def join_coeff(e):
         coeffs[e] = jnp.where(real, jnp.concatenate([halves_of[0, e], halves_of[1, e]], axis=0), 0.0)
@@ -721,23 +738,28 @@
     add_near(0)
     update(0, 4)
 
+    def ready_face(s):
+        expand(0, range(N))
+        put(0, 4, plane(0, 4))
+
+    def next_face(s):
+        send_face(s, [tot[0, 64 + n] for n in range(16)])
+
+    ready_face(1)
+    next_face(1)
+
     def step(s, _):
         cycle = s // PERIOD
         live = s < STEPS - 1
         coarse = (lax.rem(s, PERIOD) == NPRE) & live
         deferred = lax.rem(s - 1, PERIOD) != NPRE
-
         behind = deferred & (s > 1)
-
-        @pl.when(coarse)
-        def _():
-            coarse_send(cycle)
-
-        expand(0, range(N))
+        plain = jnp.logical_not(coarse) & live
+
+        expand(0, (0,))
         cross(0)
-        mine = plane(0, 4)
-        put(0, 4, mine)
-        send_face(s, mine)
+        for b in range(4):
+            put(0, b, plane(0, b))
 
         @pl.when(there(2))
         def _():
@@ -745,14 +767,13 @@
 
         @pl.when(behind)
         def _():
+            expand(1, (0,))
+            cross(1)
             for b in range(4):
                 put(1, b, plane(1, b))
                 if b:
                     update(1, b)
             update(1, 4)
-
-        for b in range(4):
-            put(0, b, plane(0, b))
 
         @pl.when(s == 1)
         def _():
@@ -768,50 +789,82 @@
                     update(1, b)
             update(1, 4)
 
-        expand(1, range(1, N))
-
-        @pl.when(deferred)
+        @pl.when(coarse)
         def _():
             add_far(s - 1)
             update(1, 0)
 
-        expand(1, (0,))
-        cross(1)
-        for n, x in enumerate(plane(1, 4)):
-            joined = tot[0, n] + x
+        expand(1, range(N))
+        put(1, 4, plane(1, 4))
+
+        @pl.when(coarse)
+        def _():
+            cross(1)
+            for b in range(4):
+                put(1, b, plane(1, b))
+
+        @pl.when(jnp.logical_not(live))
+        def _():
+            emit(sol, sol_out, False)
+
+        @pl.when(plain)
+        def _():
+            for b in range(1, 4):
+                update(0, b)
+
+        add_near(s)
+
+        @pl.when(plain)
+        def _():
+            update(0, 4)
+            ready_face(s + 1)
+
+        @pl.when(deferred & jnp.logical_not(coarse))
+        def _():
+            add_far(s - 1)
+            for n in range(16):
+                shift_top(1, 64, n)
+
+        for n in range(16):
+            joined = tot[0, n] + tot[1, 64 + n]
             tot[0, n] = joined
             tot[1, 64 + n] = joined
 
-        @pl.when(coarse)
-        def _():
-            for b in range(4):
-                put(1, b, plane(1, b))
-
-        @pl.when(jnp.logical_not(live))
-        def _():
-            emit(sol, sol_out, False)
-
-        @pl.when(jnp.logical_not(coarse))
-        def _():
-            for b in range(4):
-                update(0, b)
-
-        add_near(s)
+        @pl.when(plain)
+        def _():
+            for n in range(16):
+                shift_top(0, 64, n)
 
         @pl.when(coarse)
         def _():
             add_far(s)
             correct(cycle)
-            for b in range(4):
+            for b in range(N):
                 update(0, b)
-                update(1, b + 1)
-            update(1, 0)
-
-        update(0, 4)
+                update(1, b)
+            ready_face(s + 1)
+
+        @pl.when((lax.rem(s + 1, PERIOD) == NPRE) & (s + 1 < STEPS - 1))
+        def _():
+            coarse_send((s + 1) // PERIOD)
+
+        @pl.when(live)
+        def _():
+            next_face(s + 1)
+
         return 0
 
     lax.fori_loop(1, STEPS, step, 0)
     emit(tot, res_out, True)
+
+
+def hand_over(sol_ref, res_ref, sol_out, res_out, sems):
+    copies = [pltpu.make_async_copy(src, dst, sems.at[k]) for k, (src, dst) in enumerate(
+        ((sol_ref, sol_out), (res_ref, res_out)))]
+    for copy in copies:
+        copy.start()
+    for copy in copies:
+        copy.wait()
 
 
 def per_device(sizes, load, kappa, wet):
@@ -847,6 +900,7 @@
             pltpu.VMEM((2, nodes) + tile, F32),
             pltpu.VMEM((2, nodes) + tile, F32),
             pltpu.VMEM((2,) + tile, F32),
+            pltpu.VMEM((2, 4) + tile, F32),
             pltpu.VMEM((STEPS, messages) + tile, F32),
             pltpu.VMEM((2, STEPS, messages) + tile, F32),
             pltpu.VMEM((CYCLES, SPAN, 2) + tile, F32),
@@ -857,6 +911,12 @@
         compiler_params=pltpu.CompilerParams(collective_id=0, has_side_effects=True, vmem_limit_bytes=16 * 2 ** 20),
     )(*[pltpu.with_memory_space_constraint(x, pltpu.HBM) for x in (
         load.reshape(nodes, layers, width), kappa.reshape(layers, width), wet.reshape(layers, width))])
+    place = pl.BlockSpec(memory_space=pl.ANY)
+    solution, residual = pl.pallas_call(
+        hand_over, out_shape=(out, out), in_specs=[place] * 2, out_specs=(place, place),
+        scratch_shapes=[dma((2,))],
+        compiler_params=pltpu.CompilerParams(vmem_limit_bytes=2 ** 20),
+    )(solution, residual)
     return solution.reshape(load.shape), residual.reshape(load.shape)
 
 

time: 39.1 us -> 37.8 us (0.967)
  local copies, waits for them, and re-layouts: 1.4 us -> 0 us
    unnamed x2 -> x0, local copies, waits for them, and re-layouts: 1.4 us -> none
    pallas_call x0 -> x1, Pallas kernels: none -> 0.8 us  [per_device(): pl.pallas_call(hand_over, out_shape=(out, out), in_specs=[place] * 2, out...]
    pallas_call x1, Pallas kernels: 36.9 us -> 36.2 us  [per_device(): pl.pallas_call(functools.partial(kernel, sizes), out_shape=(out, out), in...]
where the time goes in v5:
time: 37.8 us; the launch traced here: 37.6 us
  Pallas kernels  37 us (98%)
  between operations  0.64 us (2%)
    pallas_call x1, Pallas kernels, per_device(): pl.pallas_call(functools.partial(kernel, sizes), out_shape=(out, out), in...  36.2 us
    pallas_call x1, Pallas kernels, per_device(): pl.pallas_call(hand_over, out_shape=(out, out), in_specs=[place] * 2, out...  0.8 us

profile of v5, /device:TPU:4, one launch (start us, length us, event | category | flops | bytes accessed | tf_op | source)
XLA Modules:
  0.0 37.6 jit_solution(17431757371318725900)
XLA Ops:
  0.6 36.2 %shard_map.50 = (f32[125,4,128]{2,1,0:T(4,128)S(1)}, f32[125,4,128]{2,1,0:T(4,128)S(1)}) custom-call(f32[125,4,128]{2,1,0:T(4,128)} %bitcast.9, f32[4,128]{1,0:T(4,128)} %bitcast.10, s32[4,128]{1,0:T(4,128)} %bitcast.11), custom_call_target="tpu_custom_call" | custom-call | tf_op jit(solution)/shard_map/pallas_call | solution.py:882
  36.8 0.8 %shard_map.51 = (f32[125,4,128]{2,1,0:T(4,128)}, f32[125,4,128]{2,1,0:T(4,128)}) custom-call(f32[125,4,128]{2,1,0:T(4,128)S(1)} %get-tuple-element.6.sol_ref, f32[125,4,128]{2,1,0:T(4,128)S(1)} %get-tuple-element.7.res_ref), custom_call_target="tpu_custom_call" | custom-call | tf_op jit(solution)/shard_map/pallas_call | solution.py:915

commit v6 on v5

--- a/solution.py
+++ b/solution.py
@@ -230,6 +230,7 @@
     for at in (first, groups + 1):
         part[at] = pltpu.roll(mixed, layers, 0)[0:layers]
 
+    sol[...] = jnp.zeros_like(sol)
     pl.semaphore_wait(pltpu.get_barrier_semaphore(), expected)
 
     def half_copy(h, d, slot, device, source=0):
@@ -387,13 +388,24 @@
             h.append([None if low is None else low + before(high)] + [g[k][a] for k in range(1, 4)])
         return h
 
-    def top_term(r, i, k):
-        v = [xs[r, xi(b, i, k)] for b in range(N)]
-        scale = MU[i] * MU[k]
-        r0 = float(ALPHA * scale) * (v[0] + v[4] - v[2]) + float(BETA * scale) * (v[1] - v[2])
-        return r0 - float(ODD * scale) * ((v[0] - v[4]) + v[3])
-
-    def plane(r, b):
+    def slot_of(a, c):
+        return (0 if a else 2) + (0 if c else 1)
+
+    def lumped(a, c):
+        return (MU[a] if a else W0) * (MU[c] if c else W0)
+
+    def top_plane(r):
+        h = plane_image(r, 4, [[None] * N for _ in range(N)])
+        weights = [ALPHA - ODD, BETA, -ALPHA - BETA, -ODD, ALPHA + ODD]
+        out = []
+        for a in range(4):
+            for c in range(4):
+                v = [float(weights[b] * lumped(a, c)) * sol[r, st(b, a, c)] for b in range(N)]
+                line = ((v[0] + v[1]) + (v[2] + v[3])) + v[4]
+                out.append(rhs[r, st(4, a, c)] - h[a][c] - shares[r, slot_of(a, c)] * line)
+        return out
+
+    def plane_image(r, b, along_b):
         coeff = coeffs[OWN - r]
         x = [[xs[r, xi(b, i, k)] for k in range(N)] for i in range(N)]
         along_c = [line_apply(*x[i], MUB[b] * MU[i]) for i in range(N)]
@@ -402,15 +414,18 @@
         for i in range(N):
             line = []
             for k in range(N):
-                along_b = top_term(r, i, k) if b == 4 else bs[r, xi(b, i, k)]
-                terms = sorted(((b == 2, along_b), (k == 2, along_c[i][k]), (i == 2, along_a[k][i])),
+                terms = sorted(((b == 2, along_b[i][k]), (k == 2, along_c[i][k]), (i == 2, along_a[k][i])),
                                key=lambda t: t[0])
+                terms = [t for t in terms if t[1] is not None]
                 total = -terms[0][1] if terms[0][0] else terms[0][1]
                 for negative, term in terms[1:]:
                     total = total - term if negative else total + term
                 line.append(coeff * total)
             y.append(line)
-        h = gather(y)
+        return gather(y)
+
+    def plane(r, b):
+        h = plane_image(r, b, [[bs[r, xi(b, i, k)] for k in range(N)] for i in range(N)])
         return [rhs[r, st(b, a, c)] - h[a][c] for a in range(4) for c in range(4)]
 
     def put(r, b, values):
@@ -443,8 +458,8 @@
         delta = sinv[r, n] * tot[r, n]
         sol[r, n] = sol[r, n] + delta
         a, c = n // 4, n % 4
-        factor = S[4, 0] * (MU[a] if a else W0) * (MU[c] if c else W0)
-        tot[r, at + n] = tot[r, at + n] - float(factor) * shares[r, (0 if a else 2) + (0 if c else 1)] * delta
+        factor = float((ALPHA - ODD) * lumped(a, c))
+        tot[r, at + n] = tot[r, at + n] - factor * shares[r, slot_of(a, c)] * delta
 
     def join_coeff(e):
         coeffs[e] = jnp.where(real, jnp.concatenate([halves_of[0, e], halves_of[1, e]], axis=0), 0.0)
@@ -540,7 +555,7 @@
                 cgot.at[cycle, OWN], cgot.at[cycle, slot_at(d)], c_send.at[REACH + d], c_recv.at[cycle, slot_at(d)],
                 place(d)).start())
 
-    def correct(cycle):
+    def correct(cycle, own_done):
         @pl.when(cycle == 0)
         def _():
             coarse_invert()
@@ -626,7 +641,7 @@
             h = ends(centre, W0, tilt)
             return [h[a][c] for a in range(4) for c in range(4)]
 
-        for i, targets in ((OWN - 2, ((1, 0),)), (OWN - 1, ((1, 64), (0, 0))), (OWN, ((0, 64),))):
+        def correct_face(i, targets):
             values = face_image(i)
             for r, at in targets:
                 for n, value in enumerate(values):
@@ -651,7 +666,8 @@
             return out
 
         at_line = {i: nodal(i) for i in (OWN - 2, OWN - 1, OWN)}
-        for r in range(2):
+
+        def correct_row(r):
             low, high = OWN - 1 - r, OWN - r
             coeff = coeffs[OWN - r]
             for kindb in range(2):
@@ -678,7 +694,14 @@
                 sol[r, n] = sol[r, n] + at_line[low][n][1]
                 sol[r, 64 + n] = sol[r, 64 + n] + at_line[high][n][1]
 
-    def emit(field, out_ref, dual):
+        correct_face(OWN - 1, ((1, 64), (0, 0)))
+        correct_face(OWN, ((0, 64),))
+        correct_row(0)
+        own_done()
+        correct_face(OWN - 2, ((1, 0),))
+        correct_row(1)
+
+    def emit(field, out_ref, dual, planes=range(N)):
         def split(mid, double, odd):
             if dual:
                 odd = float(KAPPA) * odd
@@ -697,10 +720,12 @@
                     out_ref[raw(a, b, c)] = tile[0:layers]
 
         for b in (0, 4):
-            one(b, [field[0, b * 16 + n] for n in range(16)])
-        mids = [split(field[0, 16 + n], field[0, 32 + n], field[0, 48 + n]) for n in range(16)]
-        for b in range(1, 4):
-            one(b, [v[b - 1] for v in mids])
+            if b in planes:
+                one(b, [field[0, b * 16 + n] for n in range(16)])
+        if 1 in planes:
+            mids = [split(field[0, 16 + n], field[0, 32 + n], field[0, 48 + n]) for n in range(16)]
+            for b in range(1, 4):
+                one(b, [v[b - 1] for v in mids])
 
     halo_copy(0).wait()
     for b in (4, 0, 1, 2, 3):
@@ -708,7 +733,6 @@
         put(0, b, [rhs[0, b * 16 + n] for n in range(16)])
         if b == 4:
             send_face(0, [tot[0, 64 + n] for n in range(16)])
-    sol[...] = jnp.zeros_like(sol)
     half_copy(1, 0, OWN, place(0, True)).wait()
     for d in SENDS:
         if d not in NEAR_SENDS:
@@ -721,7 +745,6 @@
     for e in range(OWN - 2, OWN + 2):
         join_coeff(e)
     invert()
-    restrict_load()
 
     @pl.when(there(-1))
     def _():
@@ -739,14 +762,15 @@
     update(0, 4)
 
     def ready_face(s):
-        expand(0, range(N))
-        put(0, 4, plane(0, 4))
+        expand(0, (4,))
+        put(0, 4, top_plane(0))
 
     def next_face(s):
         send_face(s, [tot[0, 64 + n] for n in range(16)])
 
     ready_face(1)
     next_face(1)
+    restrict_load()
 
     def step(s, _):
         cycle = s // PERIOD
@@ -756,7 +780,7 @@
         behind = deferred & (s > 1)
         plain = jnp.logical_not(coarse) & live
 
-        expand(0, (0,))
+        expand(0, range(4))
         cross(0)
         for b in range(4):
             put(0, b, plane(0, b))
@@ -767,7 +791,7 @@
 
         @pl.when(behind)
         def _():
-            expand(1, (0,))
+            expand(1, range(4))
             cross(1)
             for b in range(4):
                 put(1, b, plane(1, b))
@@ -775,6 +799,43 @@
                     update(1, b)
             update(1, 4)
 
+        @pl.when(coarse)
+        def _():
+            add_far(s - 1)
+            update(1, 0)
+
+        @pl.when(s > 1)
+        def _():
+            expand(1, (4,))
+            put(1, 4, top_plane(1))
+
+        @pl.when(coarse)
+        def _():
+            expand(1, range(4))
+            cross(1)
+            for b in range(4):
+                put(1, b, plane(1, b))
+
+        @pl.when(jnp.logical_not(live))
+        def _():
+            emit(sol, sol_out, False)
+
+        @pl.when(plain)
+        def _():
+            for b in range(1, 4):
+                update(0, b)
+
+        add_near(s)
+
+        @pl.when(jnp.logical_not(live))
+        def _():
+            emit(tot, res_out, True, range(1, N))
+
+        @pl.when(plain)
+        def _():
+            update(0, 4)
+            ready_face(s + 1)
+
         @pl.when(s == 1)
         def _():
             @pl.when(there(-1))
@@ -788,74 +849,64 @@
                 if b:
                     update(1, b)
             update(1, 4)
-
-        @pl.when(coarse)
-        def _():
-            add_far(s - 1)
-            update(1, 0)
-
-        expand(1, range(N))
-        put(1, 4, plane(1, 4))
-
-        @pl.when(coarse)
-        def _():
-            cross(1)
-            for b in range(4):
-                put(1, b, plane(1, b))
-
-        @pl.when(jnp.logical_not(live))
-        def _():
-            emit(sol, sol_out, False)
-
-        @pl.when(plain)
-        def _():
-            for b in range(1, 4):
-                update(0, b)
-
-        add_near(s)
-
-        @pl.when(plain)
-        def _():
-            update(0, 4)
-            ready_face(s + 1)
-
-        @pl.when(deferred & jnp.logical_not(coarse))
+            expand(1, (4,))
+            put(1, 4, top_plane(1))
+
+        def join(n):
+            joined = tot[0, n] + tot[1, 64 + n]
+            tot[0, n] = joined
+            tot[1, 64 + n] = joined
+
+        @pl.when(deferred & plain)
         def _():
             add_far(s - 1)
             for n in range(16):
                 shift_top(1, 64, n)
-
-        for n in range(16):
-            joined = tot[0, n] + tot[1, 64 + n]
-            tot[0, n] = joined
-            tot[1, 64 + n] = joined
+                join(n)
+                shift_top(0, 64, n)
+
+        @pl.when(jnp.logical_not(deferred & plain))
+        def _():
+            @pl.when(deferred & jnp.logical_not(coarse))
+            def _():
+                add_far(s - 1)
+                for n in range(16):
+                    shift_top(1, 64, n)
+
+            for n in range(16):
+                join(n)
+
+            @pl.when(plain)
+            def _():
+                for n in range(16):
+                    shift_top(0, 64, n)
+
+        @pl.when(coarse)
+        def _():
+            add_far(s)
+
+            def own_done():
+                for b in range(N):
+                    update(0, b)
+                ready_face(s + 1)
+                next_face(s + 1)
+
+            correct(cycle, own_done)
+            for b in range(N):
+                update(1, b)
+
+        @pl.when((lax.rem(s + 1, PERIOD) == NPRE) & (s + 1 < STEPS - 1))
+        def _():
+            coarse_send((s + 1) // PERIOD)
 
         @pl.when(plain)
         def _():
-            for n in range(16):
-                shift_top(0, 64, n)
-
-        @pl.when(coarse)
-        def _():
-            add_far(s)
-            correct(cycle)
-            for b in range(N):
-                update(0, b)
-                update(1, b)
-            ready_face(s + 1)
-
-        @pl.when((lax.rem(s + 1, PERIOD) == NPRE) & (s + 1 < STEPS - 1))
-        def _():
-            coarse_send((s + 1) // PERIOD)
-
-        @pl.when(live)
-        def _():
             next_face(s + 1)
 
         return 0
 
     lax.fori_loop(1, STEPS, step, 0)
-    emit(tot, res_out, True)
+    emit(tot, res_out, True, (0,))
 
 
 def hand_over(sol_ref, res_ref, sol_out, res_out, sems):

time: 37.8 us -> 37.4 us (0.989)
  Pallas kernels: 37 us -> 36.6 us
    pallas_call x1, Pallas kernels: 36.2 us -> 35.8 us  [per_device(): pl.pallas_call(functools.partial(kernel, sizes), out_shape=(out, out), in...]
where the time goes in v6:
time: 37.4 us; the launch traced here: 37.2 us
  Pallas kernels  36.6 us (98%)
  between operations  0.64 us (2%)
    pallas_call x1, Pallas kernels, per_device(): pl.pallas_call(functools.partial(kernel, sizes), out_shape=(out, out), in...  35.8 us
    pallas_call x1, Pallas kernels, per_device(): pl.pallas_call(hand_over, out_shape=(out, out), in_specs=[place] * 2, out...  0.8 us

profile of v6, /device:TPU:4, one launch (start us, length us, event | category | flops | bytes accessed | tf_op | source)
XLA Modules:
  0.0 37.2 jit_solution(8255819958647901481)
XLA Ops:
  0.6 35.8 %shard_map.50 = (f32[125,4,128]{2,1,0:T(4,128)S(1)}, f32[125,4,128]{2,1,0:T(4,128)S(1)}) custom-call(f32[125,4,128]{2,1,0:T(4,128)} %bitcast.9, f32[4,128]{1,0:T(4,128)} %bitcast.10, s32[4,128]{1,0:T(4,128)} %bitcast.11), custom_call_target="tpu_custom_call" | custom-call | tf_op jit(solution)/shard_map/pallas_call | solution.py:933
  36.4 0.8 %shard_map.51 = (f32[125,4,128]{2,1,0:T(4,128)}, f32[125,4,128]{2,1,0:T(4,128)}) custom-call(f32[125,4,128]{2,1,0:T(4,128)S(1)} %get-tuple-element.6.sol_ref, f32[125,4,128]{2,1,0:T(4,128)S(1)} %get-tuple-element.7.res_ref), custom_call_target="tpu_custom_call" | custom-call | tf_op jit(solution)/shard_map/pallas_call | solution.py:966

commit v7 on v6

--- a/solution.py
+++ b/solution.py
@@ -60,7 +60,7 @@
 CS = (SC[0, 0] - SC[0, 1]) / 2
 CE, CO = (WC[0, 0] + WC[0, 1]) / 2, (WC[0, 0] - WC[0, 1]) / 2
 C1, C2, C3 = CS * CE * CE, 2 * CS * CO * CE, 3 * CS * CO * CO
-SENDS = [d for d in range(-REACH + 1, REACH + 1) if d != 0]
+SENDS = sorted((d for d in range(-REACH + 1, REACH + 1) if d != 0), key=abs)
 RECVS = [d for d in range(-REACH, REACH) if d != 0]
 NEAR_SENDS = [-1, 1, 2]
 NEAR_RECVS = [-1, 1, -2]
@@ -337,11 +337,12 @@
 
     def send_face(s, values):
         pack(s, values)
+
+        @pl.when(there(2) & (s < STEPS - 1))
+        def _():
+            far_copy(s).start()
+
         near_copy(s).start()
-
-        @pl.when(there(2) & (s < STEPS - 1))
-        def _():
-            far_copy(s).start()
 
     def add_near(s):
         near_copy(s).wait()

time: 37.4 us -> 36.7 us (0.981)
  Pallas kernels: 36.6 us -> 35.9 us
    pallas_call x1, Pallas kernels: 35.8 us -> 35.1 us  [per_device(): pl.pallas_call(functools.partial(kernel, sizes), out_shape=(out, out), in...]
where the time goes in v7:
time: 36.7 us; the launch traced here: 36.5 us
  Pallas kernels  35.9 us (98%)
  between operations  0.64 us (2%)
    pallas_call x1, Pallas kernels, per_device(): pl.pallas_call(functools.partial(kernel, sizes), out_shape=(out, out), in...  35.1 us
    pallas_call x1, Pallas kernels, per_device(): pl.pallas_call(hand_over, out_shape=(out, out), in_specs=[place] * 2, out...  0.8 us

profile of v7, /device:TPU:4, one launch (start us, length us, event | category | flops | bytes accessed | tf_op | source)
XLA Modules:
  0.0 36.5 jit_solution(4704921358788838883)
XLA Ops:
  0.6 35.1 %shard_map.50 = (f32[125,4,128]{2,1,0:T(4,128)S(1)}, f32[125,4,128]{2,1,0:T(4,128)S(1)}) custom-call(f32[125,4,128]{2,1,0:T(4,128)} %bitcast.9, f32[4,128]{1,0:T(4,128)} %bitcast.10, s32[4,128]{1,0:T(4,128)} %bitcast.11), custom_call_target="tpu_custom_call" | custom-call | tf_op jit(solution)/shard_map/pallas_call | solution.py:934
  35.7 0.8 %shard_map.51 = (f32[125,4,128]{2,1,0:T(4,128)}, f32[125,4,128]{2,1,0:T(4,128)}) custom-call(f32[125,4,128]{2,1,0:T(4,128)S(1)} %get-tuple-element.6.sol_ref, f32[125,4,128]{2,1,0:T(4,128)S(1)} %get-tuple-element.7.res_ref), custom_call_target="tpu_custom_call" | custom-call | tf_op jit(solution)/shard_map/pallas_call | solution.py:967
